TPU v7x, 32 devices: a whole 2x2x4 slice. The times are simulated.
32 devices in a mesh: stream: 2 (over y), dp: 16 (over z, x, core).
Axes of the slice: x: 2, y: 2, z: 4, core: 2. Of those that a mesh axis runs over, the one named last changes fastest.
Arguments:
- tokens: bfloat16 [2, 16384, 768], P('stream', 'dp'), may hold values from -40 to 40, as said below
- first_gain: float32 [2, 768], P('stream'), may hold values from 0.25 to 1.75
- first_shift: float32 [2, 768], P('stream'), may hold values from -1.5 to 1.5
- query_weight: bfloat16 [2, 768, 768], P('stream'), may hold values from -0.21875 to 0.21875
- query_bias: float32 [2, 768], P('stream'), may hold values from -1.5 to 1.5
- key_weight: bfloat16 [2, 768, 768], P('stream'), may hold values from -0.21875 to 0.21875
- value_weight: bfloat16 [2, 768, 768], P('stream'), may hold values from -0.21875 to 0.21875
- value_bias: float32 [2, 768], P('stream'), may hold values from -0.5 to 0.5
- out_weight: bfloat16 [2, 768, 768], P('stream'), may hold values from -1.75 to 1.75
- out_bias: float32 [2, 768], P('stream'), may hold values from -1.5 to 1.5
- second_gain: float32 [2, 768], P('stream'), may hold values from 0.25 to 1.75
- second_shift: float32 [2, 768], P('stream'), may hold values from -1.5 to 1.5
- up_weight: bfloat16 [2, 768, 3072], P('stream'), may hold values from -0.21875 to 0.21875
- up_bias: float32 [2, 3072], P('stream'), may hold values from -1.5 to 1.5
- down_weight: bfloat16 [2, 3072, 768], P('stream'), may hold values from -0.109375 to 0.109375
- down_bias: float32 [2, 768], P('stream'), may hold values from -1.5 to 1.5
- box_table: float32 [2, 768], P('stream'), may hold values from -4 to 4
- segments: int32 [2, 32, 512], P(None, 'dp'), may hold values from 0 to 63, never falling along the last dimension, each value on 1 to 16 neighbouring positions
- validity: int32 [2, 32, 512], P(None, 'dp'), may hold values from 0 to 1, as said below
- seg_boxes: int32 [32, 64, 4], P('dp'), may hold values from 0 to 1023
- cotangent: bfloat16 [2, 16384, 768], P('stream', 'dp'), may hold values from -6 to 6
Outputs:
- layer_out: bfloat16 [2, 16384, 768], P('stream', 'dp')
- grad_tokens: float32 [2, 16384, 768], P('stream', 'dp')
- grad_first_gain: float32 [2, 768], P('stream', 'dp')
- grad_first_shift: float32 [2, 768], P('stream', 'dp')
- grad_query_weight: float32 [2, 768, 768], P('stream', 'dp')
- grad_query_bias: float32 [2, 768], P('stream', 'dp')
- grad_key_weight: float32 [2, 768, 768], P('stream', 'dp')
- grad_value_weight: float32 [2, 768, 768], P('stream', 'dp')
- grad_value_bias: float32 [2, 768], P('stream', 'dp')
- grad_out_weight: float32 [2, 768, 768], P('stream', 'dp')
- grad_out_bias: float32 [2, 768], P('stream', 'dp')
- grad_second_gain: float32 [2, 768], P('stream', 'dp')
- grad_second_shift: float32 [2, 768], P('stream', 'dp')
- grad_up_weight: float32 [2, 768, 3072], P('stream', 'dp')
- gradient_expand_bias: float32 [2, 3072], P('stream', 'dp')
- grad_down_weight: float32 [2, 3072, 768], P('stream', 'dp')
- grad_down_bias: float32 [2, 768], P('stream', 'dp')
- grad_box_table: float32 [2, 768], P('stream', 'dp')
- root_means: float32 [2, 3], P('stream')
Inputs may be any that keep to these rules, and one draw needn't show every extreme that they name: `tokens`: activations of both streams. `validity`: in each page of each stream the valid tokens come first, 256 of them or more. `segments`: within a page of a stream the segment numbers never fall; a segment spans 1 to 16 tokens.
All inputs are finite; a program needn't handle non-finite values.
Results may differ from a plain program's by a relative error of at most 0.012.
The roundings to bfloat16 on the way count: a program that leaves them out, or rounds other values in their place, can miss the bound.
Values may be sent and summed in bfloat16 or wider, within the bound.
No kernel may reach another device: no remote copies, remote signals or barrier semaphores. Data moves between devices by JAX's collectives and lax.ppermute only.
A program may use at most 192 MiB of HBM per device.

v0:
```python
import jax
import jax.numpy as jnp
from jax import lax
from jax.sharding import PartitionSpec as P

HEADS = 12
BUCKETS = 32


score_scale = 0.125
norm_eps = 1e-05
mask_fill = -1000000000.0
box_step = 32
precise_variant = lax.Precision.HIGHEST


def swapped(value, axis, distance):
    mask = 2**distance
    pairs = [(source, source ^ mask) for source in range(lax.axis_size(axis))]
    return lax.ppermute(value, axis, pairs)


def norm_rows(value_rows, gain, shift):
    centre = value_rows - jnp.mean(value_rows, -1, keepdims=True)
    spread = jnp.mean(centre * centre, -1, keepdims=True)
    return centre * lax.rsqrt(spread + norm_eps) * gain + shift


def precise_gelu_value(value_rows):
    return jax.nn.gelu(value_rows, approximate=False)


def pick_stream(pair, stream):
    return jnp.where(stream == 0, pair[0], pair[1])


def leading(array):
    return array[None]


def column_sums(array):
    return jnp.sum(array.astype(jnp.float32), 0)


def box_onehots(seg_boxes, buckets):
    half = buckets // 2
    levels = jnp.arange(buckets, dtype=jnp.int32)
    centre_x = (seg_boxes[..., 0] + seg_boxes[..., 2]) // 2
    centre_y = (seg_boxes[..., 1] + seg_boxes[..., 3]) // 2
    step_x = (
        jnp.clip((centre_x[:, None, :] - centre_x[:, :, None]) // box_step, -half, half - 1) + half
    )
    step_y = (
        jnp.clip((centre_y[:, None, :] - centre_y[:, :, None]) // box_step, -half, half - 1) + half
    )
    return (
        (step_x[..., None] == levels).astype(jnp.float32),
        (step_y[..., None] == levels).astype(jnp.float32),
    )


def page_scores(query, keys, seg_bias, own_seg, far_seg, far_keep):
    seg_levels = jnp.arange(seg_bias.shape[-1], dtype=jnp.int32)
    hot_query = (own_seg[:, None] == seg_levels[None, :]).astype(jnp.bfloat16)
    hot_key = (far_seg[:, None] == seg_levels[None, :]).astype(jnp.bfloat16)
    picked = jnp.einsum(
        "is,hst->hit", hot_query, seg_bias, preferred_element_type=jnp.float32
    ).astype(jnp.bfloat16)
    bias = jnp.einsum("hit,jt->hij", picked, hot_key, preferred_element_type=jnp.float32)
    raw = (
        jnp.einsum("ihe,jhe->hij", query, keys, preferred_element_type=jnp.float32) * score_scale
        + bias
    )
    return (jnp.where(far_keep[None, None, :] > 0, raw, mask_fill), hot_query, hot_key)


def attend_page(block):
    query, keys, value_rows, seg_bias, own_seg, far_seg, far_keep = block
    scores, hot_query, hot_key = page_scores(query, keys, seg_bias, own_seg, far_seg, far_keep)
    peak_score = jnp.max(scores, -1, keepdims=True)
    raised = jnp.exp(scores - peak_score)
    denominator = jnp.sum(raised, -1, keepdims=True)
    probs = (raised / denominator).astype(jnp.bfloat16)
    mixed = jnp.einsum("hij,jhe->ihe", probs, value_rows, preferred_element_type=jnp.float32)
    return (mixed.reshape(mixed.shape[0], -1), (peak_score + jnp.log(denominator))[..., 0])


def attend_back(block):
    query, keys, value_rows, seg_bias, own_seg, far_seg, far_keep, grad_mixed, log_total = block
    scores, hot_query, hot_key = page_scores(query, keys, seg_bias, own_seg, far_seg, far_keep)
    probs = jnp.exp(scores - log_total[..., None])
    length = query.shape[0]
    grad_heads = grad_mixed.reshape(length, query.shape[1], -1)
    grad_probs = jnp.einsum(
        "ihe,jhe->hij", grad_heads, value_rows, preferred_element_type=jnp.float32
    )
    gradient_score_matrix = (
        probs * (grad_probs - jnp.sum(probs * grad_probs, -1, keepdims=True))
    ).astype(jnp.bfloat16)
    grad_values = jnp.einsum(
        "hij,ihe->jhe", probs.astype(jnp.bfloat16), grad_heads, preferred_element_type=jnp.float32
    )
    grad_query = (
        jnp.einsum("hij,jhe->ihe", gradient_score_matrix, keys, preferred_element_type=jnp.float32)
        * score_scale
    )
    grad_keys = (
        jnp.einsum("hij,ihe->jhe", gradient_score_matrix, query, preferred_element_type=jnp.float32)
        * score_scale
    )
    key_sums = jnp.einsum(
        "hij,jt->hit", gradient_score_matrix, hot_key, preferred_element_type=jnp.float32
    )
    grad_bias = jnp.einsum(
        "is,hit->hst", hot_query.astype(jnp.float32), key_sums, precision=precise_variant
    )
    return (
        grad_query.reshape(length, -1),
        grad_keys.reshape(length, -1),
        grad_values.reshape(length, -1),
        grad_bias,
    )


def body(
    tokens,
    first_gain,
    first_shift,
    query_weight,
    query_bias,
    key_weight,
    value_weight,
    value_bias,
    out_weight,
    out_bias,
    second_gain,
    second_shift,
    up_weight,
    up_bias,
    down_weight,
    down_bias,
    box_table,
    segments,
    validity,
    seg_boxes,
    cotangent,
):
    stream = lax.axis_index("stream")
    width = tokens.shape[2]
    pages = segments.shape[1]
    page_len = segments.shape[2]
    length = pages * page_len
    own_seg = pick_stream(segments, stream)
    far_seg = pick_stream(segments, 1 - stream)
    own_keep = pick_stream(validity, stream)
    far_keep = pick_stream(validity, 1 - stream)
    inputs = tokens[0].astype(jnp.float32)
    normed = norm_rows(inputs, first_gain[0], first_shift[0])
    normed_low = normed.astype(jnp.bfloat16)
    query = (
        jnp.dot(normed_low, query_weight[0], preferred_element_type=jnp.float32) + query_bias[0]
    ).astype(jnp.bfloat16)
    keys = jnp.dot(normed_low, key_weight[0], preferred_element_type=jnp.float32).astype(
        jnp.bfloat16
    )
    value_rows = (
        jnp.dot(normed_low, value_weight[0], preferred_element_type=jnp.float32) + value_bias[0]
    ).astype(jnp.bfloat16)
    far_keys, far_values = swapped((keys, value_rows), "stream", 0)
    hot_x, hot_y = box_onehots(seg_boxes, BUCKETS)
    tables = box_table[0].reshape(2, HEADS, BUCKETS)
    seg_bias = (
        jnp.einsum("pabn,hn->phab", hot_x, tables[0], precision=precise_variant)
        + jnp.einsum("pabn,hn->phab", hot_y, tables[1], precision=precise_variant)
    ).astype(jnp.bfloat16)

    def split_heads(array):
        return array.reshape(pages, page_len, HEADS, -1)

    mixed, log_total = lax.map(
        attend_page,
        (
            split_heads(query),
            split_heads(far_keys),
            split_heads(far_values),
            seg_bias,
            own_seg,
            far_seg,
            far_keep,
        ),
    )
    mixed_low = mixed.reshape(length, width).astype(jnp.bfloat16)
    branch = jnp.dot(mixed_low, out_weight[0], preferred_element_type=jnp.float32) + out_bias[0]
    middle = inputs + branch
    normed_two = norm_rows(middle, second_gain[0], second_shift[0])
    normed_two_low = normed_two.astype(jnp.bfloat16)
    hidden = jnp.dot(normed_two_low, up_weight[0], preferred_element_type=jnp.float32) + up_bias[0]
    activated = precise_gelu_value(hidden).astype(jnp.bfloat16)
    feed = jnp.dot(activated, down_weight[0], preferred_element_type=jnp.float32) + down_bias[0]
    output = middle + feed
    token_weight = own_keep.reshape(length, 1).astype(jnp.float32)
    squares = jnp.stack(
        [
            jnp.sum(output * output * token_weight),
            jnp.sum(branch * branch * token_weight),
            jnp.sum(feed * feed * token_weight),
        ]
    )
    totals, counted = lax.psum((squares, jnp.sum(own_keep).astype(jnp.float32)), "dp")
    root_means = jnp.sqrt(totals / (counted * width) + 1e-06).reshape(1, 3)
    grad_out = cotangent[0].astype(jnp.float32)
    grad_feed = grad_out.astype(jnp.bfloat16)
    grad_down_weight = jnp.einsum(
        "tf,td->fd", activated, grad_feed, preferred_element_type=jnp.float32
    )
    grad_down_bias = column_sums(grad_feed)
    grad_activated = jnp.einsum(
        "td,fd->tf", grad_feed, down_weight[0], preferred_element_type=jnp.float32
    )
    gelu_value, gelu_pull = jax.vjp(precise_gelu_value, hidden)
    grad_hidden = gelu_pull(grad_activated)[0].astype(jnp.bfloat16)
    grad_up_weight = jnp.einsum(
        "td,tf->df", normed_two_low, grad_hidden, preferred_element_type=jnp.float32
    )
    gradient_expand_bias = column_sums(grad_hidden)
    grad_normed_two = jnp.einsum(
        "tf,df->td", grad_hidden, up_weight[0], preferred_element_type=jnp.float32
    )
    second_value, second_pull = jax.vjp(norm_rows, middle, second_gain[0], second_shift[0])
    grad_mid_norm, grad_second_gain, grad_second_shift = second_pull(grad_normed_two)
    grad_middle = grad_out + grad_mid_norm
    grad_branch = grad_middle.astype(jnp.bfloat16)
    grad_out_weight = jnp.einsum(
        "td,te->de", mixed_low, grad_branch, preferred_element_type=jnp.float32
    )
    grad_out_bias = column_sums(grad_branch)
    grad_mixed = jnp.einsum(
        "te,de->td", grad_branch, out_weight[0], preferred_element_type=jnp.float32
    ).astype(jnp.bfloat16)
    grad_query_pages, grad_far_keys, grad_far_values, grad_bias = lax.map(
        attend_back,
        (
            split_heads(query),
            split_heads(far_keys),
            split_heads(far_values),
            seg_bias,
            own_seg,
            far_seg,
            far_keep,
            grad_mixed.reshape(pages, page_len, width),
            log_total,
        ),
    )
    grad_query = grad_query_pages.reshape(length, width).astype(jnp.bfloat16)
    sent_keys = grad_far_keys.reshape(length, width).astype(jnp.bfloat16)
    sent_values = grad_far_values.reshape(length, width).astype(jnp.bfloat16)
    grad_keys, grad_values = swapped((sent_keys, sent_values), "stream", 0)
    grad_query_weight = jnp.einsum(
        "td,te->de", normed_low, grad_query, preferred_element_type=jnp.float32
    )
    grad_query_bias = column_sums(grad_query)
    grad_key_weight = jnp.einsum(
        "td,te->de", normed_low, grad_keys, preferred_element_type=jnp.float32
    )
    grad_value_weight = jnp.einsum(
        "td,te->de", normed_low, grad_values, preferred_element_type=jnp.float32
    )
    grad_value_bias = column_sums(grad_values)
    grad_normed = (
        jnp.einsum("te,de->td", grad_query, query_weight[0], preferred_element_type=jnp.float32)
        + jnp.einsum("te,de->td", grad_keys, key_weight[0], preferred_element_type=jnp.float32)
        + jnp.einsum("te,de->td", grad_values, value_weight[0], preferred_element_type=jnp.float32)
    )
    first_value, first_pull = jax.vjp(norm_rows, inputs, first_gain[0], first_shift[0])
    grad_in_norm, grad_first_gain, grad_first_shift = first_pull(grad_normed)
    grad_tokens = grad_middle + grad_in_norm
    grad_table = jnp.concatenate(
        [
            jnp.einsum("pabn,phab->hn", hot_x, grad_bias, precision=precise_variant),
            jnp.einsum("pabn,phab->hn", hot_y, grad_bias, precision=precise_variant),
        ],
        0,
    ).reshape(1, -1)
    (
        sum_first_gain,
        total_leading_offset,
        sum_query_weight,
        sum_query_bias,
        sum_key_weight,
        sum_value_weight,
        total_value_offset_bias,
        sum_out_weight,
        sum_out_bias,
        sum_box_table,
        sum_second_gain,
        sum_second_shift,
        sum_up_weight,
        sum_up_bias,
        sum_down_weight,
        sum_down_bias,
    ) = (
        lax.psum_scatter(leading(grad_first_gain), "dp", scatter_dimension=1, tiled=True),
        lax.psum_scatter(leading(grad_first_shift), "dp", scatter_dimension=1, tiled=True),
        lax.psum_scatter(leading(grad_query_weight), "dp", scatter_dimension=1, tiled=True),
        lax.psum_scatter(leading(grad_query_bias), "dp", scatter_dimension=1, tiled=True),
        lax.psum_scatter(leading(grad_key_weight), "dp", scatter_dimension=1, tiled=True),
        lax.psum_scatter(leading(grad_value_weight), "dp", scatter_dimension=1, tiled=True),
        lax.psum_scatter(leading(grad_value_bias), "dp", scatter_dimension=1, tiled=True),
        lax.psum_scatter(leading(grad_out_weight), "dp", scatter_dimension=1, tiled=True),
        lax.psum_scatter(leading(grad_out_bias), "dp", scatter_dimension=1, tiled=True),
        lax.psum_scatter(grad_table, "dp", scatter_dimension=1, tiled=True),
        lax.psum_scatter(leading(grad_second_gain), "dp", scatter_dimension=1, tiled=True),
        lax.psum_scatter(leading(grad_second_shift), "dp", scatter_dimension=1, tiled=True),
        lax.psum_scatter(leading(grad_up_weight), "dp", scatter_dimension=1, tiled=True),
        lax.psum_scatter(leading(gradient_expand_bias), "dp", scatter_dimension=1, tiled=True),
        lax.psum_scatter(leading(grad_down_weight), "dp", scatter_dimension=1, tiled=True),
        lax.psum_scatter(leading(grad_down_bias), "dp", scatter_dimension=1, tiled=True),
    )
    return (
        leading(output.astype(jnp.bfloat16)),
        leading(grad_tokens),
        sum_first_gain,
        total_leading_offset,
        sum_query_weight,
        sum_query_bias,
        sum_key_weight,
        sum_value_weight,
        total_value_offset_bias,
        sum_out_weight,
        sum_out_bias,
        sum_second_gain,
        sum_second_shift,
        sum_up_weight,
        sum_up_bias,
        sum_down_weight,
        sum_down_bias,
        sum_box_table,
        root_means,
    )


def solution(mesh):
    in_specs = (
        P("stream", "dp", None),
        P("stream", None),
        P("stream", None),
        P("stream", None, None),
        P("stream", None),
        P("stream", None, None),
        P("stream", None, None),
        P("stream", None),
        P("stream", None, None),
        P("stream", None),
        P("stream", None),
        P("stream", None),
        P("stream", None, None),
        P("stream", None),
        P("stream", None, None),
        P("stream", None),
        P("stream", None),
        P(None, "dp", None),
        P(None, "dp", None),
        P("dp", None, None),
        P("stream", "dp", None),
    )
    out_specs = (
        P("stream", "dp", None),
        P("stream", "dp", None),
        P("stream", "dp"),
        P("stream", "dp"),
        P("stream", "dp", None),
        P("stream", "dp"),
        P("stream", "dp", None),
        P("stream", "dp", None),
        P("stream", "dp"),
        P("stream", "dp", None),
        P("stream", "dp"),
        P("stream", "dp"),
        P("stream", "dp"),
        P("stream", "dp", None),
        P("stream", "dp"),
        P("stream", "dp", None),
        P("stream", "dp"),
        P("stream", "dp"),
        P("stream", None),
    )
    return jax.shard_map(body, mesh=mesh, in_specs=in_specs, out_specs=out_specs, check_vma=False)
```

profile of v0, /device:TPU:0, one launch (start us, length us, event | category | flops | bytes accessed | tf_op | source)
XLA Modules:
  0.0 1479.0 jit_solution(329772398643674627)
XLA Ops:
  43.1 10.7 collective-permute-done.1
  63.1 23.5 %collective-permute-done = bf16[1024,768]{1,0:T(8,128)(2,1)} collective-permute-done((bf16[1024,768]{1,0:T(8,128)(2,1)}, bf16[1024,768]{1,0:T(8,128)(2,1)}, u32[]{:S(2)}, u32[]{:S(2)}) %collective-permute-start) | collective-permute-done | bytes 1572896 | tf_op jit(solution)/shard_map/ppermute | solution.py:20
  97.4 64.0 %while.28 = (s32[]{:T(128)}, bf16[2,512,768]{2,1,0:T(8,128)(2,1)}, f32[2,12,512]{2,1,0:T(8,128)}, bf16[2,512,12,64]{1,3,2,0:T(8,128)(2,1)}, s32[2,512]{1,0:T(2,1...) while((s32[]{:T(128)}, bf16[2,512,768]{2,1,0:T(8,128)(2,1)}, ...), condition=%wide.region_5.6_spmd, body=%wide.region_2.5_spmd.sunk | while | flops 1287055872 | bytes 119955616 | solution.py:180
  97.4 7.5 fusion.210
  104.9 8.9 fusion.211
  113.8 6.6 fusion.212
  129.4 7.5 fusion.210
  136.9 8.9 fusion.211
  145.8 6.6 fusion.212
  161.4 5.8 fusion.139
  168.0 36.0 %multiply_convert_fusion.1 = (bf16[1024,3072]{1,0:T(8,128)(2,1)}, f32[1024,3072]{1,0:T(8,128)}, f32[1024,3072]{1,0:T(8,128)}) fusion(f32[3072]{0:T(1024)S(1)} %bitcast.421, bf16[1,768,3072]{2,1,0:T(8,128)(2,1)S(1)} %bitcast.420, f32[1024,768]{0,1:T(8,128)S(1)} %get-tuple-element.352, f32[768]{0:T(1024)S(1)} %copy-done.62, f32[768]{0:T(1024)S(1)} %copy-done.50, ...), kind=kOutput, calls=%fused_computation.83 | convolution fusion | flops 5043388416 | bytes 39348224 | tf_op jit(solution)/shard_map/dot_general | solution.py:197
  204.0 17.4 %convert_reduce_fusion = (f32[3072]{0:T(1024)}, bf16[1024,3072]{1,0:T(8,128)(2,1)}) fusion(f32[1024,3072]{1,0:T(8,128)} %get-tuple-element.350, bf16[1,3072,768]{2,1,0:T(8,128)(2,1)} %param.39, bf16[1,1024,768]{2,1,0:T(8,128)(2,1)S(1)} %copy-done.18, f32[1024,3072]{1,0:T(8,128)} %get-tuple-element.376, f32[3072]{0:T(1024)S(1)} %bitcast.422), kind=kOutput, calls=%fused_computation.81 | convolution fusion | flops 4885312512 | bytes 37773312 | tf_op jit(solution)/shard_map/td,fd->tf/dot_general | solution.py:217
  221.4 10.7 fusion.150
  235.7 13.7 multiply_reduce_fusion.3
  258.4 129.0 %while.29 = (s32[]{:T(128)}, bf16[2,512,768]{2,1,0:T(8,128)(2,1)}, bf16[2,512,768]{2,1,0:T(8,128)(2,1)}, bf16[2,512,768]{2,1,0:T(8,128)(2,1)}, f32[2,12,64,64]{2...) while((s32[]{:T(128)}, bf16[2,512,768]{2,1,0:T(8,128)(2,1)}, ...), condition=%wide.region_12.13_spmd, body=%wide.region_10.12_spmd.sunk | while | flops 3204442624 | bytes 235090320 | solution.py:240
  260.9 7.5 fusion.230
  268.5 6.3 fusion.231
  274.8 13.5 multiply_reduce_fusion.8
  288.4 12.6 multiply_convert_fusion.3
  305.6 4.8 convolution_multiply_fusion.5
  325.2 7.5 fusion.230
  332.8 6.3 fusion.231
  339.1 13.5 multiply_reduce_fusion.8
  352.6 12.6 multiply_convert_fusion.3
  369.9 4.8 convolution_multiply_fusion.5
  404.5 20.6 %collective-permute-done.2 = bf16[1024,768]{1,0:T(8,128)(2,1)} collective-permute-done((bf16[1024,768]{1,0:T(8,128)(2,1)}, bf16[1024,768]{1,0:T(8,128)(2,1)}, u32[]{:S(2)}, u32[]{:S(2)}) %collective-permute-start.2) | collective-permute-done | bytes 1572896 | tf_op jit(solution)/shard_map/ppermute | solution.py:20
  428.0 29.1 %collective-permute-done.3 = bf16[1024,768]{1,0:T(8,128)(2,1)} collective-permute-done((bf16[1024,768]{1,0:T(8,128)(2,1)}, bf16[1024,768]{1,0:T(8,128)(2,1)}, u32[]{:S(2)}, u32[]{:S(2)}) %collective-permute-start.3) | collective-permute-done | bytes 1572896 | tf_op jit(solution)/shard_map/ppermute | solution.py:20
  472.1 4.7 convolution_bitcast_fusion.3
  476.9 4.4 convolution_bitcast_fusion.6
  481.4 4.5 convolution_bitcast_fusion.4
  486.0 4.4 convolution_bitcast_fusion.5
  490.5 10.6 convolution_bitcast_fusion.2
  502.5 10.2 convolution_bitcast_fusion.1
  515.5 32.0 %all-reduce = (f32[3]{0:T(128)S(1)}, f32[]{:T(128)}) all-reduce(f32[3]{0:T(128)S(1)} %pad_maximum_fusion.1, f32[]{:T(128)S(6)} %convert_element_type.172), channel_id=1, replica_groups=mesh['stream'=2,'dp'=16] {'dp'}, use_global_device_ids=true, to_apply=%region_43.44 | all-reduce | flops 4 | bytes 32 | tf_op jit(solution)/shard_map/psum | solution.py:209
  552.9 10.0 reduce-scatter.57.cloned.1.call-done
  564.3 57.0 %reduce-scatter.67.cloned.1.call-done = f32[48,1]{1,0:T(8,128)} async-done(((f32[768,1]{1,0:T(8,128)}), f32[48,1]{1,0:T(8,128)}) %reduce-scatter.67.cloned.1.call-update) | async-done | bytes 208
  622.6 56.6 %reduce-scatter.53.cloned.1.call-done = f32[48,1]{1,0:T(8,128)} async-done(((f32[768,1]{1,0:T(8,128)}), f32[48,1]{1,0:T(8,128)}) %reduce-scatter.53.cloned.1.call-update) | async-done | bytes 208
  680.6 61.3 %reduce-scatter.63.cloned.1.call-done = f32[192,1]{1,0:T(8,128)} async-done(((f32[3072,1]{1,0:T(8,128)}), f32[192,1]{1,0:T(8,128)}) %reduce-scatter.63.cloned.1.call-update) | async-done | bytes 784
  747.0 52.9 %reduce-scatter.55.cloned.1.call-done = f32[48,1]{1,0:T(8,128)} async-done(((f32[768,1]{1,0:T(8,128)}), f32[48,1]{1,0:T(8,128)}) %reduce-scatter.55.cloned.1.call-update) | async-done | bytes 208
  801.2 57.2 %reduce-scatter.65.cloned.1.call-done = f32[48,1]{1,0:T(8,128)} async-done(((f32[768,1]{1,0:T(8,128)}), f32[48,1]{1,0:T(8,128)}) %reduce-scatter.65.cloned.1.call-update) | async-done | bytes 208
  859.8 56.7 %reduce-scatter.49.cloned.1.call-done = f32[48,1]{1,0:T(8,128)} async-done(((f32[768,1]{1,0:T(8,128)}), f32[48,1]{1,0:T(8,128)}) %reduce-scatter.49.cloned.1.call-update) | async-done | bytes 208
  917.8 57.0 %reduce-scatter.51.cloned.1.call-done = f32[48,1]{1,0:T(8,128)} async-done(((f32[768,1]{1,0:T(8,128)}), f32[48,1]{1,0:T(8,128)}) %reduce-scatter.51.cloned.1.call-update) | async-done | bytes 208
  976.2 65.1 %reduce-scatter.43.cloned.1.call-done = f32[1,48,768]{2,1,0:T(8,128)} async-done(((f32[1,768,768]{2,1,0:T(8,128)}), f32[1,48,768]{2,1,0:T(8,128)}) %reduce-scatter.43.cloned.1.call-update) | async-done | bytes 147472 | tf_op jit(solution)/shard_map/reduce_scatter | solution.py:309
  1041.2 66.7 %reduce-scatter.37.cloned.1.call-done = f32[1,48,768]{2,1,0:T(8,128)} async-done(((f32[1,768,768]{2,1,0:T(8,128)}), f32[1,48,768]{2,1,0:T(8,128)}) %reduce-scatter.37.cloned.1.call-update) | async-done | bytes 147472 | tf_op jit(solution)/shard_map/reduce_scatter | solution.py:304
  1107.9 66.3 %reduce-scatter.41.cloned.1.call-done = f32[1,48,768]{2,1,0:T(8,128)} async-done(((f32[1,768,768]{2,1,0:T(8,128)}), f32[1,48,768]{2,1,0:T(8,128)}) %reduce-scatter.41.cloned.1.call-update) | async-done | bytes 147472 | tf_op jit(solution)/shard_map/reduce_scatter | solution.py:307
  1174.2 66.7 %reduce-scatter.39.cloned.1.call-done = f32[1,48,768]{2,1,0:T(8,128)} async-done(((f32[1,768,768]{2,1,0:T(8,128)}), f32[1,48,768]{2,1,0:T(8,128)}) %reduce-scatter.39.cloned.1.call-update) | async-done | bytes 147472 | tf_op jit(solution)/shard_map/reduce_scatter | solution.py:306
  1240.9 114.9 %reduce-scatter.45.cloned.1.call-done = f32[1,48,3072]{2,1,0:T(8,128)} async-done(((f32[1,768,3072]{2,1,0:T(8,128)}), f32[1,48,3072]{2,1,0:T(8,128)}) %reduce-scatter.45.cloned.1.call-update) | async-done | bytes 589840 | tf_op jit(solution)/shard_map/reduce_scatter | solution.py:314
  1355.8 116.2 %reduce-scatter.47.cloned.1.call-done = f32[1,192,768]{2,1,0:T(8,128)} async-done(((f32[1,3072,768]{2,1,0:T(8,128)}), f32[1,192,768]{2,1,0:T(8,128)}) %reduce-scatter.47.cloned.1.call-update) | async-done | bytes 589840 | tf_op jit(solution)/shard_map/reduce_scatter | solution.py:316
  (351 shorter events, 183.1 us)
Async XLA Ops:
  7.2 154.2 %copy-start = (bf16[1,768,768]{2,1,0:T(8,128)(2,1)S(1)}, bf16[1,768,768]{2,1,0:T(8,128)(2,1)}, u32[]{:S(2)}) copy-start(bf16[1,768,768]{2,1,0:T(8,128)(2,1)} %param.33) | copy-start | bytes 3538948
  7.2 543.1 %reduce-scatter.61.cloned.1.call-start = ((), (), s32[]{:S(2)}) async-start(), calls=%async_computation.28 | async-start | bytes 417792
  8.0 22.4 %copy-start.37 = (f32[768]{0:T(1024)}, f32[768]{0:T(1024)S(1)}, u32[]{:S(2)}) copy-start(f32[768]{0:T(1024)S(1)} %reduce.5) | copy-start | bytes 9220
  8.8 21.7 %copy-start.60 = (f32[768]{0:T(1024)}, f32[768]{0:T(1024)S(1)}, u32[]{:S(2)}) copy-start(f32[768]{0:T(1024)S(1)} %reduce.6) | copy-start | bytes 9220
  10.5 20.0 %copy-start.8 = (bf16[1,1024,768]{1,2,0:T(8,128)(2,1)}, bf16[1,1024,768]{1,2,0:T(8,128)(2,1)S(1)}, u32[]{:S(2)}) copy-start(bf16[1,1024,768]{1,2,0:T(8,128)(2,1)S(1)} %copy.110) | copy-start | bytes 4718596
  10.8 19.7 %copy-start.29 = (f32[1024]{0:T(1024)}, f32[1024]{0:T(1024)S(1)}, u32[]{:S(2)}) copy-start(f32[1024]{0:T(1024)S(1)} %broadcast_multiply_fusion.1) | copy-start | bytes 12292
  12.3 18.1 %copy-start.39 = (f32[1024]{0:T(1024)}, f32[1024]{0:T(1024)S(1)}, u32[]{:S(2)}) copy-start(f32[1024]{0:T(1024)S(1)} %fusion.126) | copy-start | bytes 12292
  15.2 38.5 %collective-permute-start.1 = (bf16[1024,768]{1,0:T(8,128)(2,1)}, bf16[1024,768]{1,0:T(8,128)(2,1)}, u32[]{:S(2)}, u32[]{:S(2)}) collective-permute-start(bf16[1024,768]{1,0:T(8,128)(2,1)} %convolution_convert_fusion.3), channel_id=1, source_target_pairs={{0,16},{16,0},{1,17},{17,1},{2,18},{18,2},{3,19},{19,3},{4,20},{20... | collective-permute-start | bytes 4718600 | tf_op jit(solution)/shard_map/ppermute | solution.py:20
  22.5 64.2 %collective-permute-start = (bf16[1024,768]{1,0:T(8,128)(2,1)}, bf16[1024,768]{1,0:T(8,128)(2,1)}, u32[]{:S(2)}, u32[]{:S(2)}) collective-permute-start(bf16[1024,768]{1,0:T(8,128)(2,1)} %add_convert_fusion.3), channel_id=1, source_target_pairs={{0,16},{16,0},{1,17},{17,1},{2,18},{18,2},{3,19},{19,3},{4,20},{20... | collective-permute-start | bytes 4718600 | tf_op jit(solution)/shard_map/ppermute | solution.py:20
  97.4 64.0 %copy-start.52 = (f32[768]{0:T(1024)S(1)}, f32[768]{0:T(1024)}, u32[]{:S(2)}) copy-start(f32[768]{0:T(1024)} %reduce.11) | copy-start | bytes 9220
  167.2 36.8 %copy-start.10 = (f32[1024,768]{0,1:T(8,128)}, f32[1024,768]{0,1:T(8,128)S(1)}, u32[]{:S(2)}) copy-start(f32[1024,768]{0,1:T(8,128)S(1)} %get-tuple-element.352) | copy-start | bytes 9437188
  167.3 82.2 %copy-start.43 = (f32[1024]{0:T(1024)}, f32[1024]{0:T(1024)S(1)}, u32[]{:S(2)}) copy-start(f32[1024]{0:T(1024)S(1)} %broadcast_multiply_fusion) | copy-start | bytes 12292
  167.7 81.8 %copy-start.48 = (f32[1024]{0:T(1024)}, f32[1024]{0:T(1024)S(1)}, u32[]{:S(2)}) copy-start(f32[1024]{0:T(1024)S(1)} %fusion.127) | copy-start | bytes 12292
  168.0 36.0 %copy-start.18 = (bf16[1,1024,768]{2,1,0:T(8,128)(2,1)S(1)}, bf16[1,1024,768]{2,1,0:T(8,128)(2,1)}, u32[]{:S(2)}) copy-start(bf16[1,1024,768]{2,1,0:T(8,128)(2,1)} %param.45) | copy-start | bytes 4718596
  235.7 13.7 copy-start.11
  235.7 13.8 copy-start.16
  258.4 130.9 %copy-start.57 = (f32[768]{0:T(1024)S(1)}, f32[768]{0:T(1024)}, u32[]{:S(2)}) copy-start(f32[768]{0:T(1024)} %get-tuple-element.378) | copy-start | bytes 9220
  258.4 131.9 %copy-start.56 = (f32[768]{0:T(1024)S(1)}, f32[768]{0:T(1024)}, u32[]{:S(2)}) copy-start(f32[768]{0:T(1024)} %get-tuple-element.289) | copy-start | bytes 9220
  258.4 133.2 %copy-start.47 = (f32[768]{0:T(1024)S(1)}, f32[768]{0:T(1024)}, u32[]{:S(2)}) copy-start(f32[768]{0:T(1024)} %get-tuple-element.345) | copy-start | bytes 9220
  288.4 14.1 copy-start.2
  352.6 14.1 copy-start.2
  387.5 8.5 copy-start.26
  387.5 37.7 %collective-permute-start.2 = (bf16[1024,768]{1,0:T(8,128)(2,1)}, bf16[1024,768]{1,0:T(8,128)(2,1)}, u32[]{:S(2)}, u32[]{:S(2)}) collective-permute-start(bf16[1024,768]{1,0:T(8,128)(2,1)} %bitcast.395), channel_id=1, source_target_pairs={{0,16},{16,0},{1,17},{17,1},{2,18},{18,2},{3,19},{19,3},{4,20},{20... | collective-permute-start | bytes 4718600 | tf_op jit(solution)/shard_map/ppermute | solution.py:20
  390.2 161.3 %reduce-scatter.59.cloned.1.call-start = ((), (), s32[]{:S(2)}) async-start(), calls=%async_computation.27 | async-start | bytes 417792
  391.2 65.9 %collective-permute-start.3 = (bf16[1024,768]{1,0:T(8,128)(2,1)}, bf16[1024,768]{1,0:T(8,128)(2,1)}, u32[]{:S(2)}, u32[]{:S(2)}) collective-permute-start(bf16[1024,768]{1,0:T(8,128)(2,1)} %bitcast.394), channel_id=1, source_target_pairs={{0,16},{16,0},{1,17},{17,1},{2,18},{18,2},{3,19},{19,3},{4,20},{20... | collective-permute-start | bytes 4718600 | tf_op jit(solution)/shard_map/ppermute | solution.py:20
  391.5 171.4 %reduce-scatter.57.cloned.1.call-start = ((), (), s32[]{:S(2)}) async-start(), calls=%async_computation.26 | async-start | bytes 417792
  394.6 226.6 %reduce-scatter.67.cloned.1.call-start = ((), (), s32[]{:S(2)}) async-start(), calls=%async_computation.31 | async-start | bytes 417792
  398.5 280.7 %reduce-scatter.53.cloned.1.call-start = ((), (), s32[]{:S(2)}) async-start(), calls=%async_computation.24 | async-start | bytes 417792
  399.8 342.0 %reduce-scatter.63.cloned.1.call-start = ((), (), s32[]{:S(2)}) async-start(), calls=%async_computation.29 | async-start | bytes 1671168
  401.6 398.3 %reduce-scatter.55.cloned.1.call-start = ((), (), s32[]{:S(2)}) async-start(), calls=%async_computation.25 | async-start | bytes 417792
  401.7 23.5 %copy-start.73 = (bf16[1,768,768]{2,1,0:T(8,128)(2,1)S(1)}, bf16[1,768,768]{2,1,0:T(8,128)(2,1)}, u32[]{:S(2)}) copy-start(bf16[1,768,768]{2,1,0:T(8,128)(2,1)} %param.30) | copy-start | bytes 3538948
  404.5 52.6 %copy-start.9 = (bf16[1,1024,768]{1,2,0:T(8,128)(2,1)S(1)}, bf16[1,1024,768]{1,2,0:T(8,128)(2,1)}, u32[]{:S(2)}) copy-start(bf16[1,1024,768]{1,2,0:T(8,128)(2,1)} %copy-done.8) | copy-start | bytes 4718596
  404.5 52.6 %copy-start.22 = (bf16[1,768,768]{2,1,0:T(8,128)(2,1)S(1)}, bf16[1,768,768]{2,1,0:T(8,128)(2,1)}, u32[]{:S(2)}) copy-start(bf16[1,768,768]{2,1,0:T(8,128)(2,1)} %param.31) | copy-start | bytes 3538948
  404.5 52.6 %copy-start.30 = (f32[1024]{0:T(1024)S(1)}, f32[1024]{0:T(1024)}, u32[]{:S(2)}) copy-start(f32[1024]{0:T(1024)} %copy-done.29) | copy-start | bytes 12292
  404.5 52.6 %copy-start.38 = (f32[768]{0:T(1024)S(1)}, f32[768]{0:T(1024)}, u32[]{:S(2)}) copy-start(f32[768]{0:T(1024)} %copy-done.37) | copy-start | bytes 9220
  428.0 32.5 %copy-start.46 = (f32[1024]{0:T(1024)S(1)}, f32[1024]{0:T(1024)}, u32[]{:S(2)}) copy-start(f32[1024]{0:T(1024)} %copy-done.45) | copy-start | bytes 12292
  428.0 32.5 %copy-start.40 = (f32[1024]{0:T(1024)S(1)}, f32[1024]{0:T(1024)}, u32[]{:S(2)}) copy-start(f32[1024]{0:T(1024)} %copy-done.39) | copy-start | bytes 12292
  468.8 389.7 %reduce-scatter.65.cloned.1.call-start = ((), (), s32[]{:S(2)}) async-start(), calls=%async_computation.30 | async-start | bytes 417792
  469.8 446.7 %reduce-scatter.49.cloned.1.call-start = ((), (), s32[]{:S(2)}) async-start(), calls=%async_computation.22 | async-start | bytes 417792
  470.8 504.1 %reduce-scatter.51.cloned.1.call-start = ((), (), s32[]{:S(2)}) async-start(), calls=%async_computation.23 | async-start | bytes 417792
  471.8 569.4 %reduce-scatter.43.cloned.1.call-start = ((), (), s32[]{:S(2)}) async-start(), calls=%async_computation.19 | async-start | bytes 2506752 | tf_op jit(solution)/shard_map/reduce_scatter | solution.py:309
  476.8 631.1 %reduce-scatter.37.cloned.1.call-start = ((), (), s32[]{:S(2)}) async-start(), calls=%async_computation.16 | async-start | bytes 2506752 | tf_op jit(solution)/shard_map/reduce_scatter | solution.py:304
  481.4 692.9 %reduce-scatter.41.cloned.1.call-start = ((), (), s32[]{:S(2)}) async-start(), calls=%async_computation.18 | async-start | bytes 2506752 | tf_op jit(solution)/shard_map/reduce_scatter | solution.py:307
  485.9 755.0 %reduce-scatter.39.cloned.1.call-start = ((), (), s32[]{:S(2)}) async-start(), calls=%async_computation.17 | async-start | bytes 2506752 | tf_op jit(solution)/shard_map/reduce_scatter | solution.py:306
  490.4 865.4 %reduce-scatter.45.cloned.1.call-start = ((), (), s32[]{:S(2)}) async-start(), calls=%async_computation.20 | async-start | bytes 10027008 | tf_op jit(solution)/shard_map/reduce_scatter | solution.py:314
  501.1 970.9 %reduce-scatter.47.cloned.1.call-start = ((), (), s32[]{:S(2)}) async-start(), calls=%async_computation.21 | async-start | bytes 10027008 | tf_op jit(solution)/shard_map/reduce_scatter | solution.py:316
  512.7 34.8 %copy-start.20 = (bf16[1,1024,768]{1,2,0:T(8,128)(2,1)S(1)}, bf16[1,1024,768]{1,2,0:T(8,128)(2,1)}, u32[]{:S(2)}) copy-start(bf16[1,1024,768]{1,2,0:T(8,128)(2,1)} %get-tuple-element.365) | copy-start | bytes 4718596
  743.4 728.7 %copy-start.1 = (bf16[1,768,768]{2,1,0:T(8,128)(2,1)S(1)}, bf16[1,768,768]{2,1,0:T(8,128)(2,1)}, u32[]{:S(2)}) copy-start(bf16[1,768,768]{2,1,0:T(8,128)(2,1)} %param.33) | copy-start | bytes 3538948
  (59 other events, 247.7 us)
Sparse Core Ops, SparseCore 0:
  390.4 55.8 reduce-scatter.60
  450.2 54.5 reduce-scatter.58
  508.3 54.6 reduce-scatter.56
  566.7 54.5 reduce-scatter.66
  624.6 54.5 reduce-scatter.52
  683.2 58.5 reduce-scatter.62
  745.3 54.5 reduce-scatter.54
  803.8 54.6 reduce-scatter.64
  862.0 54.4 reduce-scatter.48
  920.3 54.5 reduce-scatter.50
  979.2 61.9 reduce-scatter.42
  1045.9 61.9 reduce-scatter.36
  1112.2 61.9 reduce-scatter.40
  1178.9 61.9 reduce-scatter.38
  1245.4 110.3 reduce-scatter.44
  1360.9 111.1 reduce-scatter.46
where the time goes:
time: 1490 us; the launch traced here: 1480 us
  waiting for transfers between devices  989 us (66%)
  matrix products  272 us (18%)
  local copies, waits for them, and re-layouts  106 us (7%)
  other arithmetic  57 us (4%)
  blocking collectives  32 us (2%)
  between operations  16.7 us (1%)
    unnamed x26, waiting for transfers between devices  409 us
    reduce_scatter x1, waiting for transfers between devices, body(): lax.psum_scatter(leading(grad_down_weight), 'dp', scatter_dimension=1, ti...  116 us
    reduce_scatter x1, waiting for transfers between devices, body(): lax.psum_scatter(leading(grad_up_weight), 'dp', scatter_dimension=1, tile...  115 us
    ppermute x4, waiting for transfers between devices, swapped(): return lax.ppermute(value, axis, pairs)  83.9 us
    reduce_scatter x1, waiting for transfers between devices, body(): lax.psum_scatter(leading(grad_query_weight), 'dp', scatter_dimension=1, t...  66.7 us
    reduce_scatter x1, waiting for transfers between devices, body(): lax.psum_scatter(leading(grad_key_weight), 'dp', scatter_dimension=1, til...  66.7 us
    reduce_scatter x1, waiting for transfers between devices, body(): lax.psum_scatter(leading(grad_value_weight), 'dp', scatter_dimension=1, t...  66.3 us
    reduce_scatter x1, waiting for transfers between devices, body(): lax.psum_scatter(leading(grad_out_weight), 'dp', scatter_dimension=1, til...  65.1 us
  transfers between devices with their start and end apart: 20, of which 18 were waited for; matrix products, arithmetic and copies ran while one was open for 8% of the time, Pallas kernels for 0%

commit v1 on v0

v1 whole, which is shorter than its diff:
```python
import functools

import jax
import jax.numpy as jnp
from jax import lax
from jax.experimental import pallas as pl
from jax.experimental.pallas import tpu as pltpu
from jax.sharding import PartitionSpec as P

HEADS = 12
BUCKETS = 32

score_scale = 0.125
norm_eps = 1e-05
mask_fill = -1000000000.0
box_step = 32
precise_variant = lax.Precision.HIGHEST
f32 = jnp.float32
bf16 = jnp.bfloat16
VMEM_BYTES = 60 * 1024 * 1024


def nn(a, b):
    return lax.dot_general(a, b, (((1,), (0,)), ((), ())), preferred_element_type=f32)


def nt(a, b):
    return lax.dot_general(a, b, (((1,), (1,)), ((), ())), preferred_element_type=f32)


def tn(a, b):
    return lax.dot_general(a, b, (((0,), (0,)), ((), ())), preferred_element_type=f32)


def normal_rows(rows):
    centre = rows - jnp.mean(rows, -1, keepdims=True)
    spread = jnp.mean(centre * centre, -1, keepdims=True)
    scale = lax.rsqrt(spread + norm_eps)
    return centre * scale, scale


def params(**kw):
    return pltpu.CompilerParams(vmem_limit_bytes=VMEM_BYTES, **kw)


def cost(flops, moved, trans=0):
    return pl.CostEstimate(flops=int(flops), bytes_accessed=int(moved), transcendentals=int(trans))


def full(shape):
    zeros = (0,) * len(shape)
    return pl.BlockSpec(shape, lambda *_: zeros)


def query_kernel(x_ref, gain_ref, shift_ref, w_ref, b_ref, n_ref, q_ref):
    norm, _ = normal_rows(x_ref[...].astype(f32))
    low = (norm * gain_ref[...] + shift_ref[...]).astype(bf16)
    n_ref[...] = low
    query = (nn(low, w_ref[...]) + b_ref[...]).astype(bf16)
    q_ref[...] = (query.astype(f32) * score_scale).astype(bf16)


def query_call(x, gain, shift, weight, bias):
    length, width = x.shape
    tile = 256
    rows = pl.BlockSpec((tile, width), lambda i: (i, 0))
    return pl.pallas_call(
        query_kernel,
        grid=(length // tile,),
        in_specs=[rows, full((1, width)), full((1, width)), full(weight.shape), full((1, width))],
        out_specs=[rows, rows],
        out_shape=[jax.ShapeDtypeStruct(x.shape, bf16)] * 2,
        compiler_params=params(),
        cost_estimate=cost(2 * length * width * width, 6 * length * width + 2 * width * width),
        name="query",
    )(x, gain, shift, weight, bias)


def pair_kernel(x_ref, gain_ref, shift_ref, wk_ref, wv_ref, b_ref, n_ref, k_ref, v_ref):
    norm, _ = normal_rows(x_ref[...].astype(f32))
    low = (norm * gain_ref[...] + shift_ref[...]).astype(bf16)
    n_ref[...] = low
    k_ref[...] = nn(low, wk_ref[...]).astype(bf16)
    v_ref[...] = (nn(low, wv_ref[...]) + b_ref[...]).astype(bf16)


def pair_call(x, gain, shift, key_weight, value_weight, bias):
    length, width = x.shape
    tile = 256
    rows = pl.BlockSpec((tile, width), lambda i: (i, 0))
    return pl.pallas_call(
        pair_kernel,
        grid=(length // tile,),
        in_specs=[
            rows,
            full((1, width)),
            full((1, width)),
            full(key_weight.shape),
            full(value_weight.shape),
            full((1, width)),
        ],
        out_specs=[rows, rows, rows],
        out_shape=[jax.ShapeDtypeStruct(x.shape, bf16)] * 3,
        compiler_params=params(),
        cost_estimate=cost(4 * length * width * width, 8 * length * width + 4 * width * width),
        name="pair",
    )(x, gain, shift, key_weight, value_weight, bias)


def head_lanes(value, head, head_dim):
    lane = lax.broadcasted_iota(jnp.int32, value.shape, 1)
    mine = (lane >= head * head_dim) & (lane < (head + 1) * head_dim)
    return jnp.where(mine, value, jnp.zeros_like(value))


def attend_kernel(q_ref, k_ref, v_ref, bias_ref, hq_ref, hk_ref, o_ref, lse_ref):
    q, v = q_ref[...], v_ref[...]
    left = jnp.concatenate([k_ref[...], hk_ref[0]], 1)
    v_turned = v.astype(f32).T.astype(bf16)
    parts = []
    for head in range(2):
        picked = nn(hq_ref[0], bias_ref[0, head]).astype(bf16)
        right = jnp.concatenate([head_lanes(q, head, 64), picked], 1)
        scores = nt(left, right)
        peak = jnp.max(scores, 0, keepdims=True)
        raised = jnp.exp(scores - peak)
        total = jnp.sum(raised, 0, keepdims=True)
        probs = (raised * (1.0 / total)).astype(bf16)
        parts.append(nn(v_turned[head * 64 : (head + 1) * 64], probs))
        lse_ref[0, 0, head : head + 1, :] = peak + jnp.log(total)
    o_ref[...] = jnp.concatenate(parts, 0).T.astype(bf16)


def attend_specs(page_len):
    rows = pl.BlockSpec((page_len, 128), lambda p, h: (p, h))
    bias = pl.BlockSpec((1, 2, 64, 128), lambda p, h: (p, h, 0, 0))
    hot = pl.BlockSpec((1, page_len, 128), lambda p, h: (p, 0, 0))
    lse = pl.BlockSpec((1, 1, 2, page_len), lambda p, h: (p, h, 0, 0))
    return rows, bias, hot, lse


def attend_call(q, k, v, bias, hot_q, hot_k):
    length, width = q.shape
    pages, page_len = hot_q.shape[0], hot_q.shape[1]
    rows, bias_spec, hot, lse = attend_specs(page_len)
    hot64 = pl.BlockSpec((1, page_len, 64), lambda p, h: (p, 0, 0))
    return pl.pallas_call(
        attend_kernel,
        grid=(pages, width // 128),
        in_specs=[rows, rows, rows, bias_spec, hot64, hot],
        out_specs=[rows, lse],
        out_shape=[
            jax.ShapeDtypeStruct((length, width), bf16),
            jax.ShapeDtypeStruct((pages, width // 128, 2, page_len), f32),
        ],
        compiler_params=params(),
        cost_estimate=cost(
            8 * length * page_len * width, 8 * length * width, length * page_len * HEADS
        ),
        name="attend",
    )(q, k, v, bias, hot_q, hot_k)


def attend_back_kernel(
    q_ref,
    k_ref,
    v_ref,
    bias_ref,
    hq_ref,
    hk_ref,
    hkt_ref,
    lse_ref,
    o_ref,
    do_ref,
    dq_ref,
    dk_ref,
    dv_ref,
    gb_ref,
):
    q, k, v, do = q_ref[...], k_ref[...], v_ref[...], do_ref[...]
    hot_q = hq_ref[0]
    left = jnp.concatenate([k, hk_ref[0]], 1)
    k_turned = k.astype(f32).T.astype(bf16)
    overlap = do.astype(f32) * o_ref[...].astype(f32)
    row = lax.broadcasted_iota(jnp.int32, (8, 128), 0)
    lane = lax.broadcasted_iota(jnp.int32, (8, 128), 1)
    chooser = (row == lane // 64).astype(f32)
    delta = lax.dot_general(
        chooser,
        overlap,
        (((1,), (1,)), ((), ())),
        preferred_element_type=f32,
        precision=precise_variant,
    )
    parts, dk, dv = [], 0.0, 0.0
    for head in range(2):
        q_head, do_head = head_lanes(q, head, 64), head_lanes(do, head, 64)
        picked = nn(hot_q, bias_ref[0, head]).astype(bf16)
        right = jnp.concatenate([q_head, picked], 1)
        probs = jnp.exp(nt(left, right) - lse_ref[0, 0, head : head + 1, :])
        slope = nt(v, do_head)
        turn = (probs * (slope - delta[head : head + 1, :])).astype(bf16)
        dv = dv + nn(probs.astype(bf16), do_head)
        dk = dk + nn(turn, q_head)
        both = nn(jnp.concatenate([k_turned[head * 64 : (head + 1) * 64], hkt_ref[0]], 0), turn)
        parts.append(both[:64])
        sums = both[64:]
        high = sums.astype(bf16)
        rest = (sums - high.astype(f32)).astype(bf16)
        gb_ref[0, head] = nn(high, hot_q) + nn(rest, hot_q)
    dq_ref[...] = (jnp.concatenate(parts, 0) * score_scale).T.astype(bf16)
    dk_ref[...] = dk.astype(bf16)
    dv_ref[...] = dv.astype(bf16)


def attend_back_call(q, k, v, bias, hot_q, hot_k, hot_kt, lse_in, o, do):
    length, width = q.shape
    pages, page_len = hot_q.shape[0], hot_q.shape[1]
    rows, bias_spec, hot, lse = attend_specs(page_len)
    hot64 = pl.BlockSpec((1, page_len, 64), lambda p, h: (p, 0, 0))
    turned = pl.BlockSpec((1, 64, page_len), lambda p, h: (p, 0, 0))
    grad_bias = pl.BlockSpec((1, 2, 64, 64), lambda p, h: (p, h, 0, 0))
    wide = jax.ShapeDtypeStruct((length, width), bf16)
    return pl.pallas_call(
        attend_back_kernel,
        grid=(pages, width // 128),
        in_specs=[rows, rows, rows, bias_spec, hot64, hot, turned, lse, rows, rows],
        out_specs=[rows, rows, rows, grad_bias],
        out_shape=[wide, wide, wide, jax.ShapeDtypeStruct((pages, HEADS, 64, 64), f32)],
        compiler_params=params(),
        cost_estimate=cost(
            20 * length * page_len * width, 16 * length * width, length * page_len * HEADS
        ),
        name="attend_back",
    )(q, k, v, bias, hot_q, hot_k, hot_kt, lse_in, o, do)


def put_rows(scratch, keep, send, at, me, relative):
    if not relative:
        keep[pl.ds(at, scratch.shape[0]), :] = scratch[...].astype(bf16)
        return
    step = scratch.shape[0] // 16
    for place in range(16):
        owner = place ^ me
        rows = scratch[pl.ds(pl.multiple_of(owner * step, step), step), :].astype(bf16)
        target = send if place & 1 else keep
        target[(place >> 1) & 1, at + (place >> 2) * step : at + ((place >> 2) + 1) * step, :] = (
            rows
        )


def put_quarter(scratch, keep, send, at, me, relative):
    if not relative:
        keep[pl.ds(at, scratch.shape[0]), :] = scratch[...].astype(bf16)
        return
    step = scratch.shape[0] // 4
    for place in range(4):
        owner = place ^ (me & 3)
        rows = scratch[pl.ds(pl.multiple_of(owner * step, step), step), :].astype(bf16)
        target = send if place & 1 else keep
        target[place >> 1, at : at + step, :] = rows


def feed_kernel(
    me_ref,
    x_ref,
    mixed_ref,
    cot_ref,
    keep_ref,
    wo_ref,
    bo_ref,
    gain_ref,
    shift_ref,
    up_ref,
    upb_ref,
    down_ref,
    downb_ref,
    out_ref,
    gm_ref,
    gx_ref,
    upg_ref,
    small_ref,
    kept_ref,
    sent_ref,
    okept_ref,
    osent_ref,
    middle_ref,
    n2_ref,
    feed_ref,
    gn_ref,
    act_ref,
    gh_ref,
    dw_ref,
    *,
    relative,
    tile,
):
    step = pl.program_id(0)
    me = me_ref[0]
    length = x_ref.shape[0]
    tiles = length // tile

    @pl.when(step == 0)
    def _():
        small_ref[...] = jnp.zeros_like(small_ref)

        @pl.loop(0, tiles)
        def _(i):
            at = pl.ds(pl.multiple_of(i * tile, tile), tile)
            branch = nn(mixed_ref[at, :], wo_ref[...]) + bo_ref[...]
            middle = x_ref[at, :].astype(f32) + branch
            middle_ref[at, :] = middle
            norm, _ = normal_rows(middle)
            n2_ref[at, :] = (norm * gain_ref[...] + shift_ref[...]).astype(bf16)
            feed_ref[at, :] = jnp.zeros_like(middle)
            gn_ref[at, :] = jnp.zeros_like(middle)
            small_ref[5:6, :] += jnp.sum(branch * branch * keep_ref[at, :], 0, keepdims=True)

    up, down, up_bias = up_ref[...], down_ref[...], upb_ref[...]
    upg_ref[...] = jnp.zeros_like(upg_ref)

    @pl.loop(0, tiles)
    def _(i):
        at = pl.ds(pl.multiple_of(i * tile, tile), tile)
        hidden = nn(n2_ref[at, :], up) + up_bias
        gate = 0.5 * (1.0 + lax.erf(hidden * 0.7071067811865476))
        bell = jnp.exp(hidden * hidden * -0.5) * 0.3989422804014327
        act = (hidden * gate).astype(bf16)
        act_ref[at, :] = act
        gh = nt(cot_ref[at, :], down) * (gate + hidden * bell)
        gh_low = gh.astype(bf16)
        gh_ref[at, :] = gh_low
        upg_ref[...] += jnp.sum(gh_low.astype(f32), 0, keepdims=True)
        feed_ref[at, :] += nn(act, down)
        gn_ref[at, :] += nt(gh_low, up)

    dw_ref[...] = tn(n2_ref[...], gh_ref[...])
    put_rows(dw_ref, kept_ref.at[0], sent_ref.at[0], 0, me, relative)
    dw_ref[...] = tn(act_ref[...], cot_ref[...])
    put_quarter(dw_ref, kept_ref.at[0], sent_ref.at[0], 192 if relative else 768, me, relative)

    @pl.when(step == pl.num_programs(0) - 1)
    def _():
        @pl.loop(0, tiles)
        def _(i):
            at = pl.ds(pl.multiple_of(i * tile, tile), tile)
            feed = feed_ref[at, :] + downb_ref[...]
            middle = middle_ref[at, :]
            output = middle + feed
            out_ref[at, :] = output.astype(bf16)
            weight = keep_ref[at, :]
            cot = cot_ref[at, :].astype(f32)
            norm, scale = normal_rows(middle)
            grad = gn_ref[at, :]
            inner = grad * gain_ref[...]
            grad_middle = cot + scale * (
                inner
                - jnp.mean(inner, -1, keepdims=True)
                - norm * jnp.mean(inner * norm, -1, keepdims=True)
            )
            gm_ref[at, :] = grad_middle
            low = grad_middle.astype(bf16)
            gh_ref[at, :] = low
            gx_ref[at, :] = nt(low, wo_ref[...]).astype(bf16)
            small_ref[0:1, :] += jnp.sum(low.astype(f32), 0, keepdims=True)
            small_ref[1:2, :] += jnp.sum(grad * norm, 0, keepdims=True)
            small_ref[2:3, :] += jnp.sum(grad, 0, keepdims=True)
            small_ref[3:4, :] += jnp.sum(cot, 0, keepdims=True)
            small_ref[4:5, :] += jnp.sum(output * output * weight, 0, keepdims=True)
            small_ref[6:7, :] += jnp.sum(feed * feed * weight, 0, keepdims=True)

        dw_ref[...] = tn(mixed_ref[...], gh_ref[...])
        put_rows(dw_ref, okept_ref, osent_ref, 0, me, relative)


def block_shapes(rows, relative, lead=()):
    if relative:
        return lead + (2, rows // 4, 768), lead + (2, rows // 4, 768)
    return lead + (rows, 768), lead + (16, 128)


def feed_call(me, x, mixed, cot, keep, wo, bo, gain, shift, up, upb, down, downb, relative):
    length, width = x.shape
    hidden = up.shape[1]
    blocks = hidden // width
    tile = 256
    rows = full((length, width))
    row = full((1, width))
    kept, sent = block_shapes(2 * width, relative)
    okept, osent = block_shapes(width, relative)
    shape = jax.ShapeDtypeStruct
    grid_spec = pltpu.PrefetchScalarGridSpec(
        num_scalar_prefetch=1,
        grid=(blocks,),
        in_specs=[
            rows,
            rows,
            rows,
            full((length, 1)),
            full((width, width)),
            row,
            row,
            row,
            pl.BlockSpec((width, width), lambda j, *_: (0, j)),
            pl.BlockSpec((1, width), lambda j, *_: (0, j)),
            pl.BlockSpec((width, width), lambda j, *_: (j, 0)),
            row,
        ],
        out_specs=[
            rows,
            rows,
            rows,
            pl.BlockSpec((1, width), lambda j, *_: (0, j)),
            full((8, width)),
            pl.BlockSpec((1,) + kept, lambda j, *_: (j,) + (0,) * len(kept)),
            pl.BlockSpec((1,) + sent, lambda j, *_: (j,) + (0,) * len(sent)),
            full(okept),
            full(osent),
        ],
        scratch_shapes=[
            pltpu.VMEM((length, width), f32),
            pltpu.VMEM((length, width), bf16),
            pltpu.VMEM((length, width), f32),
            pltpu.VMEM((length, width), f32),
            pltpu.VMEM((length, width), bf16),
            pltpu.VMEM((length, width), bf16),
            pltpu.VMEM((width, width), f32),
        ],
    )
    return pl.pallas_call(
        functools.partial(feed_kernel, relative=relative, tile=tile),
        grid_spec=grid_spec,
        out_shape=[
            shape((length, width), bf16),
            shape((length, width), f32),
            shape((length, width), bf16),
            shape((1, hidden), f32),
            shape((8, width), f32),
            shape((blocks,) + kept, bf16),
            shape((blocks,) + sent, bf16),
            shape(okept, bf16),
            shape(osent, bf16),
        ],
        compiler_params=params(),
        cost_estimate=cost(
            12 * length * width * hidden + 6 * length * width * width,
            40 * length * width,
            2 * length * hidden,
        ),
        name="feed",
    )(me, x, mixed, cot, keep, wo, bo, gain, shift, up, upb, down, downb)


def weights_kernel(
    me_ref,
    x_ref,
    xp_ref,
    n_ref,
    np_ref,
    dq_ref,
    dk_ref,
    dv_ref,
    wq_ref,
    wk_ref,
    wv_ref,
    gq_ref,
    gp_ref,
    small_ref,
    kept_ref,
    sent_ref,
    dw_ref,
    *,
    relative,
    tile,
):
    me = me_ref[0]
    length = x_ref.shape[0]
    small_ref[...] = jnp.zeros_like(small_ref)

    @pl.loop(0, length // tile)
    def _(i):
        at = pl.ds(pl.multiple_of(i * tile, tile), tile)
        dq, dk, dv = dq_ref[at, :], dk_ref[at, :], dv_ref[at, :]
        far = nt(dk, wk_ref[...]) + nt(dv, wv_ref[...])
        gp_ref[at, :] = far.astype(bf16)
        own = nt(dq, wq_ref[...])
        gq_ref[at, :] = own
        norm, _ = normal_rows(x_ref[at, :].astype(f32))
        far_norm, _ = normal_rows(xp_ref[at, :].astype(f32))
        small_ref[0:1, :] += jnp.sum(dq.astype(f32), 0, keepdims=True)
        small_ref[1:2, :] += jnp.sum(own * norm, 0, keepdims=True)
        small_ref[2:3, :] += jnp.sum(own, 0, keepdims=True)
        small_ref[3:4, :] += jnp.sum(dv.astype(f32), 0, keepdims=True)
        small_ref[4:5, :] += jnp.sum(far * far_norm, 0, keepdims=True)
        small_ref[5:6, :] += jnp.sum(far, 0, keepdims=True)

    step = 192 if relative else 768
    dw_ref[...] = tn(n_ref[...], dq_ref[...])
    put_rows(dw_ref, kept_ref, sent_ref, 0, me, relative)
    dw_ref[...] = tn(np_ref[...], dk_ref[...])
    put_rows(dw_ref, kept_ref, sent_ref, step, me, relative)
    dw_ref[...] = tn(np_ref[...], dv_ref[...])
    put_rows(dw_ref, kept_ref, sent_ref, 2 * step, me, relative)


def weights_call(me, x, xp, n, n_far, dq, dk, dv, wq, wk, wv, relative):
    length, width = x.shape
    rows, square = full((length, width)), full((width, width))
    kept, sent = block_shapes(3 * width, relative)
    shape = jax.ShapeDtypeStruct
    grid_spec = pltpu.PrefetchScalarGridSpec(
        num_scalar_prefetch=1,
        grid=(1,),
        in_specs=[rows] * 7 + [square] * 3,
        out_specs=[rows, rows, full((8, width)), full(kept), full(sent)],
        scratch_shapes=[pltpu.VMEM((width, width), f32)],
    )
    return pl.pallas_call(
        functools.partial(weights_kernel, relative=relative, tile=256),
        grid_spec=grid_spec,
        out_shape=[
            shape((length, width), f32),
            shape((length, width), bf16),
            shape((8, width), f32),
            shape(kept, bf16),
            shape(sent, bf16),
        ],
        compiler_params=params(),
        cost_estimate=cost(12 * length * width * width, 24 * length * width),
        name="weights",
    )(me, x, xp, n, n_far, dq, dk, dv, wq, wk, wv)


def tokens_kernel(x_ref, gain_ref, gm_ref, gq_ref, gf_ref, out_ref):
    norm, scale = normal_rows(x_ref[...].astype(f32))
    inner = (gq_ref[...] + gf_ref[...].astype(f32)) * gain_ref[...]
    out_ref[...] = gm_ref[...] + scale * (
        inner
        - jnp.mean(inner, -1, keepdims=True)
        - norm * jnp.mean(inner * norm, -1, keepdims=True)
    )


def tokens_call(x, gain, gm, gq, gf):
    length, width = x.shape
    rows = pl.BlockSpec((256, width), lambda i: (i, 0))
    return pl.pallas_call(
        tokens_kernel,
        grid=(length // 256,),
        in_specs=[rows, full((1, width)), rows, rows, rows],
        out_specs=rows,
        out_shape=jax.ShapeDtypeStruct((length, width), f32),
        compiler_params=params(),
        cost_estimate=cost(20 * length * width, 16 * length * width),
        name="tokens",
    )(x, gain, gm, gq, gf)


def swapped(value, axis, mask):
    pairs = [(source, source ^ mask) for source in range(lax.axis_size(axis))]
    return lax.ppermute(value, axis, pairs)


def added(a, b, dtype=bf16):
    return (a.astype(f32) + b.astype(f32)).astype(dtype)


def near_sums(kept, sent):
    half = added(kept, swapped(sent, "dp", 1))
    return added(half[0], swapped(half[1], "dp", 2))


def far_sums(value):
    other = swapped(value[1::2], "dp", 4)
    half = added(value[0::2], other)
    return added(half[0], swapped(half[1], "dp", 8), f32)


def everywhere(value):
    mask = 1
    while mask < lax.axis_size("dp"):
        value = value + swapped(value, "dp", mask)
        mask *= 2
    return value


def pick_stream(pair, stream):
    return jnp.where(stream == 0, pair[0], pair[1])


def partner_weights(stacked, me):
    low = me & 3
    piece = swapped(lax.dynamic_index_in_dim(stacked, low, 0, keepdims=False), "stream", 1)
    half = jnp.stack([piece, swapped(piece, "dp", 2)])
    whole = jnp.stack([half, swapped(half, "dp", 1)], 1).reshape(stacked.shape)
    return whole[jnp.arange(4) ^ low]


def box_onehots(seg_boxes, buckets):
    half = buckets // 2
    levels = jnp.arange(buckets, dtype=jnp.int32)
    centre_x = (seg_boxes[..., 0] + seg_boxes[..., 2]) // 2
    centre_y = (seg_boxes[..., 1] + seg_boxes[..., 3]) // 2
    step_x = (
        jnp.clip((centre_x[:, None, :] - centre_x[:, :, None]) // box_step, -half, half - 1) + half
    )
    step_y = (
        jnp.clip((centre_y[:, None, :] - centre_y[:, :, None]) // box_step, -half, half - 1) + half
    )
    return (
        (step_x[..., None] == levels).astype(jnp.float32),
        (step_y[..., None] == levels).astype(jnp.float32),
    )


def body(
    tokens,
    first_gain,
    first_shift,
    query_weight,
    query_bias,
    key_weight,
    value_weight,
    value_bias,
    out_weight,
    out_bias,
    second_gain,
    second_shift,
    up_weight,
    up_bias,
    down_weight,
    down_bias,
    box_table,
    segments,
    validity,
    seg_boxes,
    cotangent,
):
    stream = lax.axis_index("stream")
    me = lax.axis_index("dp")
    shards = lax.axis_size("dp")
    width = tokens.shape[2]
    hidden = up_weight.shape[2]
    pages, page_len = segments.shape[1], segments.shape[2]
    length = pages * page_len
    relative = shards == 16
    me_ref = me.reshape(1).astype(jnp.int32)
    x = tokens[0]

    stacked = jnp.concatenate([key_weight[0], value_weight[0]], 0).reshape(4, width // 2, width)
    far_weights = partner_weights(stacked, me).reshape(2, width, width)
    far_rows = swapped(jnp.concatenate([first_gain, first_shift, value_bias], 0), "stream", 1)
    far_x = swapped(x, "stream", 1)

    own_seg = pick_stream(segments, stream)
    far_seg = pick_stream(segments, 1 - stream)
    own_keep = pick_stream(validity, stream)
    far_keep = pick_stream(validity, 1 - stream)
    levels = jnp.arange(64, dtype=jnp.int32)
    hot_q = (own_seg[:, :, None] == levels).astype(bf16)
    hot_kt = (far_seg[:, None, :] == levels[None, :, None]).astype(bf16)
    wide_levels = jnp.arange(128, dtype=jnp.int32)
    hot_k = jnp.where(
        wide_levels == 64,
        jnp.where(far_keep[:, :, None] > 0, 0.0, mask_fill),
        (far_seg[:, :, None] == wide_levels).astype(f32),
    ).astype(bf16)
    hot_x, hot_y = box_onehots(seg_boxes, BUCKETS)
    tables = box_table[0].reshape(2, HEADS, BUCKETS)
    seg_bias = (
        jnp.einsum("pabn,hn->phab", hot_x, tables[0], precision=precise_variant)
        + jnp.einsum("pabn,hn->phab", hot_y, tables[1], precision=precise_variant)
    ).astype(bf16)
    ones = (jnp.arange(64) == 0).astype(bf16)
    seg_bias = jnp.concatenate([seg_bias, jnp.broadcast_to(ones, seg_bias.shape)], -1)

    normed, query = query_call(x, first_gain, first_shift, query_weight[0], query_bias)
    far_normed, keys, value_rows = pair_call(
        far_x, far_rows[0:1], far_rows[1:2], far_weights[0], far_weights[1], far_rows[2:3]
    )
    mixed, log_total = attend_call(query, keys, value_rows, seg_bias, hot_q, hot_k)

    keep_column = own_keep.reshape(length, 1).astype(f32)
    output, grad_middle, grad_mixed, grad_up_bias, small, kept, sent, out_kept, out_sent = (
        feed_call(
            me_ref,
            x,
            mixed,
            cotangent[0],
            keep_column,
            out_weight[0],
            out_bias,
            second_gain,
            second_shift,
            up_weight[0],
            up_bias,
            down_weight[0],
            down_bias,
            relative,
        )
    )
    blocks = hidden // width

    grad_query, grad_keys, grad_values, grad_bias = attend_back_call(
        query, keys, value_rows, seg_bias, hot_q, hot_k, hot_kt, log_total, mixed, grad_mixed
    )
    own_grad, far_grad, small_two, kept_two, sent_two = weights_call(
        me_ref,
        x,
        far_x,
        normed,
        far_normed,
        grad_query,
        grad_keys,
        grad_values,
        query_weight[0],
        far_weights[0],
        far_weights[1],
        relative,
    )
    grad_tokens = tokens_call(
        x, first_gain, grad_middle, own_grad, swapped(far_grad, "stream", 1)
    )
    grad_table = jnp.concatenate(
        [
            jnp.einsum("pabn,phba->hn", hot_x, grad_bias, precision=precise_variant),
            jnp.einsum("pabn,phba->hn", hot_y, grad_bias, precision=precise_variant),
        ],
        0,
    ).reshape(1, -1)

    back = swapped(small_two[3:6], "stream", 1)
    counted = jnp.sum(own_keep).astype(f32)
    stats = jnp.concatenate(
        [jnp.sum(small[4:7], 1), counted[None], jnp.zeros((width - 4,), f32)]
    )
    rows = jnp.concatenate(
        [
            small[0:4],
            small_two[0:1],
            small_two[1:3] + back[1:3],
            back[0:1],
            grad_table,
            grad_up_bias.reshape(blocks, width),
            stats[None],
        ],
        0,
    )
    rows = everywhere(rows)
    part = width // shards
    lanes = lax.dynamic_slice_in_dim(rows, me * part, part, 1)
    up_part = lax.dynamic_slice_in_dim(
        rows[9 : 9 + blocks].reshape(1, hidden), me * (hidden // shards), hidden // shards, 1
    )
    totals = rows[9 + blocks]
    root_means = jnp.sqrt(totals[:3] / (totals[3] * width) + 1e-06).reshape(1, 3)

    if relative:
        near = [near_sums(kept[j], sent[j]) for j in range(blocks)]
        near_out = near_sums(out_kept, out_sent)
        down_parts = jnp.stack([value[192:] for value in near])
        down_parts = down_parts[jnp.arange(4) ^ (me >> 2)]
        first = jnp.concatenate(
            [value[:192].reshape(4, 48, width) for value in near]
            + [near_out.reshape(4, 48, width), down_parts],
            1,
        )
        first = far_sums(first)
        sum_up = jnp.concatenate([first[48 * j : 48 * (j + 1)] for j in range(blocks)], 1)
        sum_out = first[48 * blocks : 48 * blocks + 48]
        sum_down = first[48 * blocks + 48 :]
        near_two = near_sums(kept_two, sent_two)
        second = jnp.concatenate(
            [near_two[192 * j : 192 * (j + 1)].reshape(4, 48, width) for j in range(3)], 1
        )
        second = far_sums(second)
        sum_query = second[:48]
        sum_pair = second[48:].astype(bf16)
    else:

        def scattered(value):
            return lax.psum_scatter(value, "dp", scatter_dimension=0, tiled=True)

        grad_up = jnp.concatenate([kept[j, :width] for j in range(blocks)], 1)
        grad_down = jnp.concatenate([kept[j, width:] for j in range(blocks)], 0)
        sum_up = scattered(grad_up.astype(f32))
        sum_down = scattered(grad_down.astype(f32))
        sum_out = scattered(out_kept.astype(f32))
        sum_query = scattered(kept_two[:width].astype(f32))
        sum_pair = jnp.concatenate(
            [
                scattered(kept_two[width : 2 * width].astype(f32)),
                scattered(kept_two[2 * width :].astype(f32)),
            ],
            0,
        ).astype(bf16)
    sum_pair = swapped(sum_pair, "stream", 1).astype(f32)
    sum_keys, sum_values = sum_pair[:part], sum_pair[part:]

    return (
        output[None],
        grad_tokens[None],
        lanes[5:6],
        lanes[6:7],
        sum_query[None],
        lanes[4:5],
        sum_keys[None],
        sum_values[None],
        lanes[7:8],
        sum_out[None],
        lanes[0:1],
        lanes[1:2],
        lanes[2:3],
        sum_up[None],
        up_part,
        sum_down[None],
        lanes[3:4],
        lanes[8:9],
        root_means,
    )


def solution(mesh):
    whole, split = P("stream", None), P("stream", "dp")
    cube, cut = P("stream", None, None), P("stream", "dp", None)
    pages = P(None, "dp", None)
    in_specs = (
        cut, whole, whole, cube, whole, cube, cube, whole, cube, whole, whole, whole,
        cube, whole, cube, whole, whole, pages, pages, P("dp", None, None), cut,
    )
    out_specs = (
        cut, cut, split, split, cut, split, cut, cut, split, cut, split, split, split,
        cut, split, cut, split, split, whole,
    )
    return jax.shard_map(body, mesh=mesh, in_specs=in_specs, out_specs=out_specs, check_vma=False)
```

time: 1490 us -> 398 us (0.27)
  waiting for transfers between devices: 989 us -> 160 us
  matrix products: 272 us -> 4.07 us
  Pallas kernels: 0 us -> 141 us
  local copies, waits for them, and re-layouts: 106 us -> 34.2 us
  blocking collectives: 32 us -> 0 us
  other arithmetic: 57 us -> 25.4 us
  starting transfers between devices: 5.99 us -> 29.3 us
    reduce_scatter x6 -> x0, waiting for transfers between devices: 496 us -> none  [the longest x1 116 us: body(): lax.psum_scatter(leading(grad_down_weight), 'dp', scatter_dimension=1, ti...]
    unnamed x26 -> x0, waiting for transfers between devices: 409 us -> none
    dot_general x42 -> x2, matrix products: 271 us -> 2.58 us  [the longest x1 1.3 us: body(): jnp.einsum('pabn,phba->hn', hot_x, grad_bias, precision=precise_variant)]
    pallas_call x0 -> x7, Pallas kernels: none -> 141 us  [the longest x1 52.1 us: feed_call(): pl.pallas_call(functools.partial(feed_kernel, relative=relative, tile=til...]
    ppermute x4 -> x28, waiting for transfers between devices: 83.9 us -> 160 us  [swapped(): return lax.ppermute(value, axis, pairs)]
    psum x1 -> x0, blocking collectives: 32 us -> none  [body(): lax.psum((squares, jnp.sum(own_keep).astype(jnp.float32)), 'dp')]
    unnamed x166 -> x41, local copies, waits for them, and re-layouts: 37.9 us -> 8.05 us
    ppermute x4 -> x28, starting transfers between devices: 5.07 us -> 29.3 us  [swapped(): return lax.ppermute(value, axis, pairs)]
  transfers between devices with their start and end apart: 20 -> 28, of which waited for: 18 -> 16; matrix products, arithmetic and copies ran while one was open for 8% -> 13% of each run, Pallas kernels for 0% -> 3%
where the time goes in v1:
time: 398 us; the launch traced here: 397 us
  waiting for transfers between devices  160 us (40%)
  Pallas kernels  141 us (35%)
  local copies, waits for them, and re-layouts  34.2 us (9%)
  starting transfers between devices  29.3 us (7%)
  other arithmetic  25.4 us (6%)
  matrix products  4.07 us (1%)
    ppermute x28, waiting for transfers between devices, swapped(): return lax.ppermute(value, axis, pairs)  160 us
    pallas_call x1, Pallas kernels, feed_call(): pl.pallas_call(functools.partial(feed_kernel, relative=relative, tile=til...  52.1 us
    pallas_call x1, Pallas kernels, attend_back_call(): pl.pallas_call(attend_back_kernel, grid=(pages, width // 128), in_specs=[...  31 us
    ppermute x28, starting transfers between devices, swapped(): return lax.ppermute(value, axis, pairs)  29.3 us
    pallas_call x1, Pallas kernels, attend_call(): pl.pallas_call(attend_kernel, grid=(pages, width // 128), in_specs=[rows,...  22.2 us
    pallas_call x1, Pallas kernels, weights_call(): pl.pallas_call(functools.partial(weights_kernel, relative=relative, tile=...  16.2 us
    convert_element_type x11, other arithmetic, added(): return (a.astype(f32) + b.astype(f32)).astype(dtype)  8.99 us
    unnamed x41, local copies, waits for them, and re-layouts  8.05 us
  transfers between devices with their start and end apart: 28, of which 16 were waited for; matrix products, arithmetic and copies ran while one was open for 13% of the time, Pallas kernels for 3%

profile of v1, /device:TPU:0, one launch (start us, length us, event | category | flops | bytes accessed | tf_op | source)
XLA Modules:
  0.0 396.6 jit_solution(18059278109305678655)
XLA Ops:
  0.7 3.0 collective-permute-start
  5.0 1.8 pad_maximum_fusion
  6.9 2.1 collective-permute-start.2
  12.0 5.5 %query.1 = (bf16[1024,768]{1,0:T(8,128)(2,1)}, bf16[1024,768]{1,0:T(8,128)(2,1)}) custom-call(bf16[1024,768]{1,0:T(8,128)(2,1)} %bitcast.174, f32[1,768]{1,0:T(1,128)} %gain_ref.5, f32[1,768]{1,0:T(1,128)} %shift_ref.2, bf16[768,768]{1,0:T(8,128)(2,1)} %bitcast.206, f32[1,768]{1,0:T(1,128)} %b_ref.1), custom_call_target="tpu_custom_call" | custom-call | flops 1207959552 | bytes 5898240 | tf_op jit(solution)/shard_map/query/pallas_call | solution.py:67
  19.1 32.1 %collective-permute-done.2 = bf16[384,768]{1,0:T(8,128)(2,1)S(1)} collective-permute-done((bf16[384,768]{1,0:T(8,128)(2,1)S(1)}, bf16[384,768]{1,0:T(8,128)(2,1)S(1)}, u32[]{:S(2)}, u32[]{:S(2)}) %collective-permute-start.2) | collective-permute-done | bytes 589856 | tf_op jit(solution)/shard_map/ppermute | solution.py:561
  51.2 1.7 collective-permute-start.3
  54.7 11.0 %collective-permute-done.3 = bf16[384,768]{1,0:T(8,128)(2,1)S(1)} collective-permute-done((bf16[384,768]{1,0:T(8,128)(2,1)S(1)}, bf16[384,768]{1,0:T(8,128)(2,1)S(1)}, u32[]{:S(2)}, u32[]{:S(2)}) %collective-permute-start.3) | collective-permute-done | bytes 589856 | tf_op jit(solution)/shard_map/ppermute | solution.py:561
  70.4 1.4 fusion.31
  71.8 1.6 pad_maximum_fusion.1
  73.4 2.4 gather_fusion
  75.8 1.6 fusion.27
  77.4 6.9 %pair.1 = (bf16[1024,768]{1,0:T(8,128)(2,1)}, bf16[1024,768]{1,0:T(8,128)(2,1)}, bf16[1024,768]{1,0:T(8,128)(2,1)}) custom-call(bf16[1024,768]{1,0:T(8,128)(2,1)} %collective-permute-done.x_ref.xp_ref, f32[1,768]{1,0:T(1,128)} %get-tuple-element.116.gain_ref, f32[1,768]{1,0:T(1,128)} %get-tuple-element.115.shift_ref, bf16[768,768]{1,0:T(8,128)(2,1)} %bitcast.190, ...), custom_call_target="tpu_custom_call" | custom-call | flops 2415919104 | bytes 8650752 | tf_op jit(solution)/shard_map/pair/pallas_call | solution.py:91
  84.3 22.2 %attend.1 = (bf16[1024,768]{1,0:T(8,128)(2,1)}, f32[2,6,2,512]{3,2,1,0:T(2,128)}) custom-call(bf16[1024,768]{1,0:T(8,128)(2,1)} %get-tuple-element.44.q_ref, bf16[1024,768]{1,0:T(8,128)(2,1)} %get-tuple-element.45.k_ref, bf16[1024,768]{1,0:T(8,128)(2,1)} %get-tuple-element.46.v_ref, bf16[2,12,64,128]{3,2,1,0:T(8,128)(2,1)} %pad_maximum_fusion.5.bias_ref, ...), custom_call_target="tpu_custom_call" | custom-call | flops 3221225472 | bytes 6291456 | tf_op jit(solution)/shard_map/attend/pallas_call | solution.py:147
  106.5 52.1 %feed.1 = (bf16[1024,768]{1,0:T(8,128)(2,1)}, f32[1024,768]{1,0:T(8,128)}, bf16[1024,768]{1,0:T(8,128)(2,1)}, f32[1,3072]{1,0:T(1,128)}, f32[8,768]{1,0:T(8,128)...) custom-call(s32[1]{0:T(128)} %bitcast.me_ref, ...), custom_call_target="tpu_custom_call" | custom-call | flops 32614907904 | bytes 31457280 | tf_op jit(solution)/shard_map/feed/pallas_call | solution.py:430
  158.6 31.0 %attend_back.1 = (bf16[1024,768]{1,0:T(8,128)(2,1)}, bf16[1024,768]{1,0:T(8,128)(2,1)}, bf16[1024,768]{1,0:T(8,128)(2,1)}, f32[2,12,64,64]{3,2,1,0:T(8,128)}) custom-call(bf16[1024,768]{1,0:T(8,128)(2,1)} %get-tuple-element.44.q_ref, bf16[1024,768]{1,0:T(8,128)(2,1)} %get-tuple-element.45.k_ref, bf16[1024,768]{1,0:T(8,128)(2,1)} %get-tuple-element.46.v_ref, ...), custom_call_target="tpu_custom_call" | custom-call | flops 8053063680 | bytes 12582912 | tf_op jit(solution)/shard_map/attend_back/pallas_call | solution.py:224
  189.6 2.1 copy.56
  194.3 16.2 %weights.1 = (f32[1024,768]{1,0:T(8,128)}, bf16[1024,768]{1,0:T(8,128)(2,1)}, f32[8,768]{1,0:T(8,128)}, bf16[2,576,768]{2,1,0:T(8,128)(2,1)}, bf16[2,576,768]{2,1,0:T(8,128)(2,1)}) custom-call(s32[1]{0:T(128)} %bitcast.me_ref, bf16[1024,768]{1,0:T(8,128)(2,1)} %bitcast.176, bf16[1024,768]{1,0:T(8,128)(2,1)} %collective-permute-done.x_ref.xp_ref, ...), custom_call_target="tpu_custom_call" | custom-call | flops 7247757312 | bytes 18874368 | tf_op jit(solution)/shard_map/weights/pallas_call | solution.py:518
  211.2 1.4 collective-permute-start.6
  217.0 1.6 collective-permute-start.8
  218.6 2.6 collective-permute-done.8
  221.2 1.6 collective-permute-start.9
  222.8 4.7 %slice_bitcast_fusion = (bf16[2,384,768]{2,1,0:T(8,128)(2,1)}, bf16[2,384,768]{2,1,0:T(8,128)(2,1)}, bf16[2,384,768]{2,1,0:T(8,128)(2,1)}, bf16[2,384,768]{2,1,0:T(8,128)(2,1)}) fusion(bf16[4,2,384,768]{3,2,1,0:T(8,128)(2,1)} %get-tuple-element.66), kind=kLoop, calls=%fused_computation.34 | loop fusion | bytes 9437184 | tf_op jit(solution)/shard_map/squeeze | solution.py:759
  228.6 2.7 collective-permute-start.10
  231.4 2.7 collective-permute-done.10
  234.7 1.5 collective-permute-start.25
  237.7 5.7 %collective-permute-done.25 = bf16[192,768]{1,0:T(8,128)(2,1)S(1)} collective-permute-done((bf16[192,768]{1,0:T(8,128)(2,1)S(1)}, bf16[192,768]{1,0:T(8,128)(2,1)S(1)}, u32[]{:S(2)}, u32[]{:S(2)}) %collective-permute-start.25) | collective-permute-done | bytes 294944 | tf_op jit(solution)/shard_map/ppermute | solution.py:561
  243.3 1.4 collective-permute-start.5
  244.9 4.2 %fusion = (bf16[2,384,768]{2,1,0:T(8,128)(2,1)S(1)}, bf16[2,384,768]{2,1,0:T(8,128)(2,1)S(1)}, bf16[2,384,768]{2,1,0:T(8,128)(2,1)S(1)}, bf16[2,384,768]{2,1,0:T(8,128)(2,1)S(1)}) fusion(bf16[2,384,768]{2,1,0:T(8,128)(2,1)S(1)} %collective-permute-done.22, bf16[4,2,384,768]{3,2,1,0:T(8,128)(2,1)} %get-tuple-element.65, ...), kind=kLoop, calls=%fused_computation.7 | loop fusion | flops 9437184 | bytes 14155776 | tf_op jit(solution)/shard_map/convert_element_type | solution.py:565
  249.2 1.6 collective-permute-start.17
  251.5 1.6 collective-permute-start.21
  253.1 12.3 %collective-permute-done.17 = bf16[384,768]{1,0:T(8,128)(2,1)S(1)} collective-permute-done((bf16[384,768]{1,0:T(8,128)(2,1)S(1)}, bf16[384,768]{1,0:T(8,128)(2,1)S(1)}, u32[]{:S(2)}, u32[]{:S(2)}) %collective-permute-start.17) | collective-permute-done | bytes 589856 | tf_op jit(solution)/shard_map/ppermute | solution.py:561
  265.4 1.5 collective-permute-start.23
  267.9 10.2 %collective-permute-done.19 = bf16[384,768]{1,0:T(8,128)(2,1)S(1)} collective-permute-done((bf16[384,768]{1,0:T(8,128)(2,1)S(1)}, bf16[384,768]{1,0:T(8,128)(2,1)S(1)}, u32[]{:S(2)}, u32[]{:S(2)}) %collective-permute-start.19) | collective-permute-done | bytes 589856 | tf_op jit(solution)/shard_map/ppermute | solution.py:561
  279.0 11.7 %collective-permute-done.21 = bf16[384,768]{1,0:T(8,128)(2,1)S(1)} collective-permute-done((bf16[384,768]{1,0:T(8,128)(2,1)S(1)}, bf16[384,768]{1,0:T(8,128)(2,1)S(1)}, u32[]{:S(2)}, u32[]{:S(2)}) %collective-permute-start.21) | collective-permute-done | bytes 589856 | tf_op jit(solution)/shard_map/ppermute | solution.py:561
  290.9 12.0 %collective-permute-done.23 = bf16[384,768]{1,0:T(8,128)(2,1)S(1)} collective-permute-done((bf16[384,768]{1,0:T(8,128)(2,1)S(1)}, bf16[384,768]{1,0:T(8,128)(2,1)S(1)}, u32[]{:S(2)}, u32[]{:S(2)}) %collective-permute-start.23) | collective-permute-done | bytes 589856 | tf_op jit(solution)/shard_map/ppermute | solution.py:561
  306.0 1.5 collective-permute-start.12
  308.2 1.6 gather_fusion.1
  316.6 11.0 %collective-permute-done.12 = bf16[576,768]{1,0:T(8,128)(2,1)} collective-permute-done((bf16[576,768]{1,0:T(8,128)(2,1)}, bf16[576,768]{1,0:T(8,128)(2,1)}, u32[]{:S(2)}, u32[]{:S(2)}) %collective-permute-start.12) | collective-permute-done | bytes 884768 | tf_op jit(solution)/shard_map/ppermute | solution.py:561
  329.9 1.6 fusion.30
  331.5 6.7 %tokens.1 = f32[1024,768]{1,0:T(8,128)} custom-call(bf16[1024,768]{1,0:T(8,128)(2,1)} %bitcast.177, f32[1,768]{1,0:T(1,128)} %gain_ref.5, f32[1024,768]{1,0:T(8,128)} %get-tuple-element.49.gm_ref, f32[1024,768]{1,0:T(8,128)} %get-tuple-element.57.gq_ref, bf16[1024,768]{1,0:T(8,128)(2,1)} %collective-permute-done.5.gf_ref), custom_call_target="tpu_custom_call" | custom-call | flops 15728640 | bytes 12582912 | tf_op jit(solution)/shard_map/tokens/pallas_call | solution.py:547
  338.1 8.0 %collective-permute-done.26 = bf16[2,432,768]{2,1,0:T(8,128)(2,1)} collective-permute-done((bf16[2,432,768]{2,1,0:T(8,128)(2,1)S(1)}, bf16[2,432,768]{2,1,0:T(8,128)(2,1)}, u32[]{:S(2)}, u32[]{:S(2)}) %collective-permute-start.26) | collective-permute-done | bytes 1327136 | tf_op jit(solution)/shard_map/ppermute | solution.py:561
  346.1 2.0 add_convert_fusion.1
  348.2 5.7 %collective-permute-done.13 = bf16[2,144,768]{2,1,0:T(8,128)(2,1)S(1)} collective-permute-done((bf16[2,144,768]{2,1,0:T(8,128)(2,1)S(1)}, bf16[2,144,768]{2,1,0:T(8,128)(2,1)S(1)}, u32[]{:S(2)}, u32[]{:S(2)}) %collective-permute-start.13) | collective-permute-done | bytes 442400 | tf_op jit(solution)/shard_map/ppermute | solution.py:561
  354.0 1.4 collective-permute-start.14
  355.5 1.6 collective-permute-start.27
  357.1 22.8 %collective-permute-done.14 = bf16[144,768]{1,0:T(8,128)(2,1)S(1)} collective-permute-done((bf16[144,768]{1,0:T(8,128)(2,1)S(1)}, bf16[144,768]{1,0:T(8,128)(2,1)S(1)}, u32[]{:S(2)}, u32[]{:S(2)}) %collective-permute-start.14) | collective-permute-done | bytes 221216 | tf_op jit(solution)/shard_map/ppermute | solution.py:561
  381.3 4.3 %collective-permute-done.15 = bf16[96,768]{1,0:T(8,128)(2,1)S(1)} collective-permute-done((bf16[96,768]{1,0:T(8,128)(2,1)S(1)}, bf16[96,768]{1,0:T(8,128)(2,1)S(1)}, u32[]{:S(2)}, u32[]{:S(2)}) %collective-permute-start.15) | collective-permute-done | bytes 147488 | tf_op jit(solution)/shard_map/ppermute | solution.py:561
  386.4 7.6 %collective-permute-done.27 = bf16[432,768]{1,0:T(8,128)(2,1)S(1)} collective-permute-done((bf16[432,768]{1,0:T(8,128)(2,1)S(1)}, bf16[432,768]{1,0:T(8,128)(2,1)S(1)}, u32[]{:S(2)}, u32[]{:S(2)}) %collective-permute-start.27) | collective-permute-done | bytes 663584 | tf_op jit(solution)/shard_map/ppermute | solution.py:561
  (156 shorter events, 42.6 us)
Async XLA Ops:
  0.7 76.7 %collective-permute-start = (bf16[1024,768]{1,0:T(8,128)(2,1)}, bf16[1024,768]{1,0:T(8,128)(2,1)}, u32[]{:S(2)}, u32[]{:S(2)}) collective-permute-start(bf16[1024,768]{1,0:T(8,128)(2,1)} %bitcast.173), channel_id=1, source_target_pairs={{0,16},{16,0},{1,17},{17,1},{2,18},{18,2},{3,19},{19,3},{4,20},{20... | collective-permute-start | bytes 4718600 | tf_op jit(solution)/shard_map/ppermute | solution.py:561
  5.0 65.4 %collective-permute-start.1 = (f32[3,768]{1,0:T(4,128)}, f32[3,768]{1,0:T(4,128)}, u32[]{:S(2)}, u32[]{:S(2)}) collective-permute-start(f32[3,768]{1,0:T(4,128)} %pad_maximum_fusion.6), channel_id=1, source_target_pairs={{0,16},{16,0},{1,17},{17,1},{2,18},{18,2},{3,19},{19,3},{4,20},{20... | collective-permute-start | bytes 27656 | tf_op jit(solution)/shard_map/ppermute | solution.py:561
  5.0 4.0 copy-start.14
  5.0 4.0 %copy-start.13 = (s32[2,64,4]{1,2,0:T(4,128)S(1)}, s32[2,64,4]{1,2,0:T(4,128)}, u32[]{:S(2)}) copy-start(s32[2,64,4]{1,2,0:T(4,128)} %param.40) | copy-start | bytes 6148
  5.0 4.2 %copy-start.10 = (s32[2,2,512]{2,1,0:T(2,128)S(1)}, s32[2,2,512]{2,1,0:T(2,128)}, u32[]{:S(2)}) copy-start(s32[2,2,512]{2,1,0:T(2,128)} %param.39) | copy-start | bytes 24580
  6.9 44.3 %collective-permute-start.2 = (bf16[384,768]{1,0:T(8,128)(2,1)S(1)}, bf16[384,768]{1,0:T(8,128)(2,1)S(1)}, u32[]{:S(2)}, u32[]{:S(2)}) collective-permute-start(bf16[384,768]{1,0:T(8,128)(2,1)S(1)} %dynamic-slice_bitcast_fusion), channel_id=1, source_target_pairs={{0,16},{16,0},{1,17},{17,1},{2,18},{18,2},{3,19},{19,3},{4,20},{20... | collective-permute-start | bytes 1769480 | tf_op jit(solution)/shard_map/ppermute | solution.py:561
  10.9 43.1 %copy-start.3 = (s32[2,64,64]{2,0,1:T(2,128)}, s32[2,64,64]{2,0,1:T(2,128)S(1)}, u32[]{:S(2)}) copy-start(s32[2,64,64]{2,0,1:T(2,128)S(1)} %clamp_add_fusion) | copy-start | bytes 98308
  51.2 14.5 %collective-permute-start.3 = (bf16[384,768]{1,0:T(8,128)(2,1)S(1)}, bf16[384,768]{1,0:T(8,128)(2,1)S(1)}, u32[]{:S(2)}, u32[]{:S(2)}) collective-permute-start(bf16[384,768]{1,0:T(8,128)(2,1)S(1)} %collective-permute-done.2), channel_id=1, source_target_pairs={{0,2},{1,3},{2,0},{3,1},{4,6},{5,7},{6,4},{7,5},{8,10},{9,11},{10,... | collective-permute-start | bytes 1769480 | tf_op jit(solution)/shard_map/ppermute | solution.py:561
  65.7 0.8 copy-start.5
  65.9 5.9 %collective-permute-start.4 = (bf16[2,384,768]{2,1,0:T(8,128)(2,1)S(1)}, bf16[2,384,768]{2,1,0:T(8,128)(2,1)S(1)}, u32[]{:S(2)}, u32[]{:S(2)}) collective-permute-start(bf16[2,384,768]{2,1,0:T(8,128)(2,1)S(1)} %get-tuple-element.91), channel_id=1, source_target_pairs={{0,1},{1,0},{2,3},{3,2},{4,5},{5,4},{6,7},{7,6},{8,9},{9,8},{10,11... | collective-permute-start | bytes 3538952 | tf_op jit(solution)/shard_map/ppermute | solution.py:561
  189.6 2.1 copy-start.4
  189.6 3.4 copy-start.6
  194.3 18.4 %copy-start.11 = (f32[8,768]{1,0:T(8,128)S(1)}, f32[8,768]{1,0:T(8,128)}, u32[]{:S(2)}) copy-start(f32[8,768]{1,0:T(8,128)} %get-tuple-element.59) | copy-start | bytes 73732
  194.3 19.9 %copy-start.12 = (f32[1,3072]{1,0:T(1,128)S(1)}, f32[1,3072]{1,0:T(1,128)}, u32[]{:S(2)}) copy-start(f32[1,3072]{1,0:T(1,128)} %get-tuple-element.62) | copy-start | bytes 36868
  194.3 21.5 %copy-start.15 = (bf16[2,192,768]{2,1,0:T(8,128)(2,1)S(1)}, bf16[2,192,768]{2,1,0:T(8,128)(2,1)}, u32[]{:S(2)}) copy-start(bf16[2,192,768]{2,1,0:T(8,128)(2,1)} %get-tuple-element.68) | copy-start | bytes 1769476
  211.2 3.7 collective-permute-start.6
  215.7 1.3 collective-permute-start.7
  215.8 12.7 %collective-permute-start.24 = (bf16[2,192,768]{2,1,0:T(8,128)(2,1)S(1)}, bf16[2,192,768]{2,1,0:T(8,128)(2,1)S(1)}, u32[]{:S(2)}, u32[]{:S(2)}) collective-permute-start(bf16[2,192,768]{2,1,0:T(8,128)(2,1)S(1)} %copy-done.15), channel_id=1, source_target_pairs={{0,1},{1,0},{2,3},{3,2},{4,5},{5,4},{6,7},{7,6},{8,9},{9,8},{10,11... | collective-permute-start | bytes 1769480 | tf_op jit(solution)/shard_map/ppermute | solution.py:561
  217.0 4.1 %collective-permute-start.8 = (f32[14,768]{1,0:T(8,128)S(1)}, f32[14,768]{1,0:T(8,128)S(1)}, u32[]{:S(2)}, u32[]{:S(2)}) collective-permute-start(f32[14,768]{1,0:T(8,128)S(1)} %add.169), channel_id=1, source_target_pairs={{0,2},{1,3},{2,0},{3,1},{4,6},{5,7},{6,4},{7,5},{8,10},{9,11},{10,... | collective-permute-start | bytes 129032 | tf_op jit(solution)/shard_map/ppermute | solution.py:561
  221.2 6.8 %collective-permute-start.9 = (f32[14,768]{1,0:T(8,128)S(1)}, f32[14,768]{1,0:T(8,128)S(1)}, u32[]{:S(2)}, u32[]{:S(2)}) collective-permute-start(f32[14,768]{1,0:T(8,128)S(1)} %add.170), channel_id=1, source_target_pairs={{0,4},{1,5},{2,6},{3,7},{4,0},{5,1},{6,2},{7,3},{8,12},{9,13},{10,... | collective-permute-start | bytes 129032 | tf_op jit(solution)/shard_map/ppermute | solution.py:561
  222.8 8.4 %copy-start.2 = (bf16[2,192,768]{2,1,0:T(8,128)(2,1)S(1)}, bf16[2,192,768]{2,1,0:T(8,128)(2,1)}, u32[]{:S(2)}) copy-start(bf16[2,192,768]{2,1,0:T(8,128)(2,1)} %get-tuple-element.67) | copy-start | bytes 1769476
  227.5 17.3 %collective-permute-start.22 = (bf16[2,384,768]{2,1,0:T(8,128)(2,1)}, bf16[2,384,768]{2,1,0:T(8,128)(2,1)S(1)}, u32[]{:S(2)}, u32[]{:S(2)}) collective-permute-start(bf16[2,384,768]{2,1,0:T(8,128)(2,1)} %get-tuple-element.79), channel_id=1, source_target_pairs={{0,1},{1,0},{2,3},{3,2},{4,5},{5,4},{6,7},{7,6},{8,9},{9,8},{10,11... | collective-permute-start | bytes 3538952 | tf_op jit(solution)/shard_map/ppermute | solution.py:561
  227.5 17.4 %collective-permute-start.20 = (bf16[2,384,768]{2,1,0:T(8,128)(2,1)}, bf16[2,384,768]{2,1,0:T(8,128)(2,1)S(1)}, u32[]{:S(2)}, u32[]{:S(2)}) collective-permute-start(bf16[2,384,768]{2,1,0:T(8,128)(2,1)} %get-tuple-element.80), channel_id=1, source_target_pairs={{0,1},{1,0},{2,3},{3,2},{4,5},{5,4},{6,7},{7,6},{8,9},{9,8},{10,11... | collective-permute-start | bytes 3538952 | tf_op jit(solution)/shard_map/ppermute | solution.py:561
  228.0 16.9 %collective-permute-start.18 = (bf16[2,384,768]{2,1,0:T(8,128)(2,1)}, bf16[2,384,768]{2,1,0:T(8,128)(2,1)}, u32[]{:S(2)}, u32[]{:S(2)}) collective-permute-start(bf16[2,384,768]{2,1,0:T(8,128)(2,1)} %get-tuple-element.81), channel_id=1, source_target_pairs={{0,1},{1,0},{2,3},{3,2},{4,5},{5,4},{6,7},{7,6},{8,9},{9,8},{10,11... | collective-permute-start | bytes 3538952 | tf_op jit(solution)/shard_map/ppermute | solution.py:561
  228.0 16.9 %collective-permute-start.16 = (bf16[2,384,768]{2,1,0:T(8,128)(2,1)}, bf16[2,384,768]{2,1,0:T(8,128)(2,1)}, u32[]{:S(2)}, u32[]{:S(2)}) collective-permute-start(bf16[2,384,768]{2,1,0:T(8,128)(2,1)} %get-tuple-element.82), channel_id=1, source_target_pairs={{0,1},{1,0},{2,3},{3,2},{4,5},{5,4},{6,7},{7,6},{8,9},{9,8},{10,11... | collective-permute-start | bytes 3538952 | tf_op jit(solution)/shard_map/ppermute | solution.py:561
  228.5 2.9 copy-start.7
  228.6 5.6 %collective-permute-start.10 = (f32[14,768]{1,0:T(8,128)S(1)}, f32[14,768]{1,0:T(8,128)S(1)}, u32[]{:S(2)}, u32[]{:S(2)}) collective-permute-start(f32[14,768]{1,0:T(8,128)S(1)} %add.171), channel_id=1, source_target_pairs={{0,8},{1,9},{2,10},{3,11},{4,12},{5,13},{6,14},{7,15},{8,0},{9,1},... | collective-permute-start | bytes 129032 | tf_op jit(solution)/shard_map/ppermute | solution.py:561
  234.1 0.6 copy-start.9
  234.7 8.6 %collective-permute-start.25 = (bf16[192,768]{1,0:T(8,128)(2,1)S(1)}, bf16[192,768]{1,0:T(8,128)(2,1)S(1)}, u32[]{:S(2)}, u32[]{:S(2)}) collective-permute-start(bf16[192,768]{1,0:T(8,128)(2,1)S(1)} %slice_bitcast_fusion.21), channel_id=1, source_target_pairs={{0,2},{1,3},{2,0},{3,1},{4,6},{5,7},{6,4},{7,5},{8,10},{9,11},{10,... | collective-permute-start | bytes 884744 | tf_op jit(solution)/shard_map/ppermute | solution.py:561
  237.1 6.3 %copy-start.8 = (f32[14,768]{1,0:T(8,128)}, f32[14,768]{1,0:T(8,128)S(1)}, u32[]{:S(2)}) copy-start(f32[14,768]{1,0:T(8,128)S(1)} %add.172) | copy-start | bytes 129028
  243.3 88.1 %collective-permute-start.5 = (bf16[1024,768]{1,0:T(8,128)(2,1)}, bf16[1024,768]{1,0:T(8,128)(2,1)}, u32[]{:S(2)}, u32[]{:S(2)}) collective-permute-start(bf16[1024,768]{1,0:T(8,128)(2,1)} %get-tuple-element.58), channel_id=1, source_target_pairs={{0,16},{16,0},{1,17},{17,1},{2,18},{18,2},{3,19},{19,3},{4,20},{20... | collective-permute-start | bytes 4718600 | tf_op jit(solution)/shard_map/ppermute | solution.py:561
  244.8 58.5 %collective-permute-start.11 = (bf16[2,576,768]{2,1,0:T(8,128)(2,1)}, bf16[2,576,768]{2,1,0:T(8,128)(2,1)S(1)}, u32[]{:S(2)}, u32[]{:S(2)}) collective-permute-start(bf16[2,576,768]{2,1,0:T(8,128)(2,1)} %get-tuple-element.64), channel_id=1, source_target_pairs={{0,1},{1,0},{2,3},{3,2},{4,5},{5,4},{6,7},{7,6},{8,9},{9,8},{10,11... | collective-permute-start | bytes 5308424 | tf_op jit(solution)/shard_map/ppermute | solution.py:561
  249.2 16.2 %collective-permute-start.17 = (bf16[384,768]{1,0:T(8,128)(2,1)S(1)}, bf16[384,768]{1,0:T(8,128)(2,1)S(1)}, u32[]{:S(2)}, u32[]{:S(2)}) collective-permute-start(bf16[384,768]{1,0:T(8,128)(2,1)S(1)} %slice_bitcast_fusion.15), channel_id=1, source_target_pairs={{0,2},{1,3},{2,0},{3,1},{4,6},{5,7},{6,4},{7,5},{8,10},{9,11},{10,... | collective-permute-start | bytes 1769480 | tf_op jit(solution)/shard_map/ppermute | solution.py:561
  250.9 27.2 %collective-permute-start.19 = (bf16[384,768]{1,0:T(8,128)(2,1)S(1)}, bf16[384,768]{1,0:T(8,128)(2,1)S(1)}, u32[]{:S(2)}, u32[]{:S(2)}) collective-permute-start(bf16[384,768]{1,0:T(8,128)(2,1)S(1)} %slice_bitcast_fusion.13), channel_id=1, source_target_pairs={{0,2},{1,3},{2,0},{3,1},{4,6},{5,7},{6,4},{7,5},{8,10},{9,11},{10,... | collective-permute-start | bytes 1769480 | tf_op jit(solution)/shard_map/ppermute | solution.py:561
  251.5 39.2 %collective-permute-start.21 = (bf16[384,768]{1,0:T(8,128)(2,1)S(1)}, bf16[384,768]{1,0:T(8,128)(2,1)S(1)}, u32[]{:S(2)}, u32[]{:S(2)}) collective-permute-start(bf16[384,768]{1,0:T(8,128)(2,1)S(1)} %slice_bitcast_fusion.11), channel_id=1, source_target_pairs={{0,2},{1,3},{2,0},{3,1},{4,6},{5,7},{6,4},{7,5},{8,10},{9,11},{10,... | collective-permute-start | bytes 1769480 | tf_op jit(solution)/shard_map/ppermute | solution.py:561
  265.4 37.5 %collective-permute-start.23 = (bf16[384,768]{1,0:T(8,128)(2,1)S(1)}, bf16[384,768]{1,0:T(8,128)(2,1)S(1)}, u32[]{:S(2)}, u32[]{:S(2)}) collective-permute-start(bf16[384,768]{1,0:T(8,128)(2,1)S(1)} %slice_bitcast_fusion.9), channel_id=1, source_target_pairs={{0,2},{1,3},{2,0},{3,1},{4,6},{5,7},{6,4},{7,5},{8,10},{9,11},{10,... | collective-permute-start | bytes 1769480 | tf_op jit(solution)/shard_map/ppermute | solution.py:561
  303.1 1.5 copy-start.1
  306.0 21.6 %collective-permute-start.12 = (bf16[576,768]{1,0:T(8,128)(2,1)}, bf16[576,768]{1,0:T(8,128)(2,1)}, u32[]{:S(2)}, u32[]{:S(2)}) collective-permute-start(bf16[576,768]{1,0:T(8,128)(2,1)} %slice_bitcast_fusion.4), channel_id=1, source_target_pairs={{0,2},{1,3},{2,0},{3,1},{4,6},{5,7},{6,4},{7,5},{8,10},{9,11},{10,... | collective-permute-start | bytes 2654216 | tf_op jit(solution)/shard_map/ppermute | solution.py:561
  309.9 1.5 copy-start
  313.9 32.2 %collective-permute-start.26 = (bf16[2,432,768]{2,1,0:T(8,128)(2,1)S(1)}, bf16[2,432,768]{2,1,0:T(8,128)(2,1)}, u32[]{:S(2)}, u32[]{:S(2)}) collective-permute-start(bf16[2,432,768]{2,1,0:T(8,128)(2,1)S(1)} %slice.331), channel_id=1, source_target_pairs={{0,4},{1,5},{2,6},{3,7},{4,0},{5,1},{6,2},{7,3},{8,12},{9,13},{10,... | collective-permute-start | bytes 3981320 | tf_op jit(solution)/shard_map/ppermute | solution.py:561
  329.1 24.7 %collective-permute-start.13 = (bf16[2,144,768]{2,1,0:T(8,128)(2,1)S(1)}, bf16[2,144,768]{2,1,0:T(8,128)(2,1)S(1)}, u32[]{:S(2)}, u32[]{:S(2)}) collective-permute-start(bf16[2,144,768]{2,1,0:T(8,128)(2,1)S(1)} %slice.295), channel_id=1, source_target_pairs={{0,4},{1,5},{2,6},{3,7},{4,0},{5,1},{6,2},{7,3},{8,12},{9,13},{10,... | collective-permute-start | bytes 1327112 | tf_op jit(solution)/shard_map/ppermute | solution.py:561
  354.0 25.9 %collective-permute-start.14 = (bf16[144,768]{1,0:T(8,128)(2,1)S(1)}, bf16[144,768]{1,0:T(8,128)(2,1)S(1)}, u32[]{:S(2)}, u32[]{:S(2)}) collective-permute-start(bf16[144,768]{1,0:T(8,128)(2,1)S(1)} %slice_bitcast_fusion.23), channel_id=1, source_target_pairs={{0,8},{1,9},{2,10},{3,11},{4,12},{5,13},{6,14},{7,15},{8,0},{9,1},... | collective-permute-start | bytes 663560 | tf_op jit(solution)/shard_map/ppermute | solution.py:561
  355.5 38.5 %collective-permute-start.27 = (bf16[432,768]{1,0:T(8,128)(2,1)S(1)}, bf16[432,768]{1,0:T(8,128)(2,1)S(1)}, u32[]{:S(2)}, u32[]{:S(2)}) collective-permute-start(bf16[432,768]{1,0:T(8,128)(2,1)S(1)} %slice_bitcast_fusion.6), channel_id=1, source_target_pairs={{0,8},{1,9},{2,10},{3,11},{4,12},{5,13},{6,14},{7,15},{8,0},{9,1},... | collective-permute-start | bytes 1990664 | tf_op jit(solution)/shard_map/ppermute | solution.py:561
  379.9 5.7 %collective-permute-start.15 = (bf16[96,768]{1,0:T(8,128)(2,1)S(1)}, bf16[96,768]{1,0:T(8,128)(2,1)S(1)}, u32[]{:S(2)}, u32[]{:S(2)}) collective-permute-start(bf16[96,768]{1,0:T(8,128)(2,1)S(1)} %slice.482), channel_id=1, source_target_pairs={{0,16},{16,0},{1,17},{17,1},{2,18},{18,2},{3,19},{19,3},{4,20},{20... | collective-permute-start | bytes 442376 | tf_op jit(solution)/shard_map/ppermute | solution.py:561

commit v2 on v1

v2 whole, which is shorter than its diff:
```python
import functools

import jax
import jax.numpy as jnp
from jax import lax
from jax.experimental import pallas as pl
from jax.experimental.pallas import tpu as pltpu
from jax.sharding import PartitionSpec as P

HEADS = 12
BUCKETS = 32
SMALL = 24

score_scale = 0.125
norm_eps = 1e-05
mask_fill = -1000000000.0
box_step = 32
precise_variant = lax.Precision.HIGHEST
f32 = jnp.float32
bf16 = jnp.bfloat16
VMEM_BYTES = 60 * 1024 * 1024


def nn(a, b):
    return lax.dot_general(a, b, (((1,), (0,)), ((), ())), preferred_element_type=f32)


def nt(a, b):
    return lax.dot_general(a, b, (((1,), (1,)), ((), ())), preferred_element_type=f32)


def tn(a, b):
    return lax.dot_general(a, b, (((0,), (0,)), ((), ())), preferred_element_type=f32)


def normal_rows(rows):
    centre = rows - jnp.mean(rows, -1, keepdims=True)
    spread = jnp.mean(centre * centre, -1, keepdims=True)
    scale = lax.rsqrt(spread + norm_eps)
    return centre * scale, scale


def params(**kw):
    return pltpu.CompilerParams(vmem_limit_bytes=VMEM_BYTES, **kw)


def cost(flops, moved, trans=0):
    return pl.CostEstimate(flops=int(flops), bytes_accessed=int(moved), transcendentals=int(trans))


def full(shape):
    zeros = (0,) * len(shape)
    return pl.BlockSpec(shape, lambda *_: zeros)


def query_kernel(x_ref, gain_ref, shift_ref, w_ref, b_ref, n_ref, q_ref):
    norm, _ = normal_rows(x_ref[...].astype(f32))
    low = (norm * gain_ref[...] + shift_ref[...]).astype(bf16)
    n_ref[...] = low
    query = (nn(low, w_ref[...]) + b_ref[...]).astype(bf16)
    q_ref[...] = (query.astype(f32) * score_scale).astype(bf16)


def query_call(x, gain, shift, weight, bias):
    length, width = x.shape
    tile = 256
    rows = pl.BlockSpec((tile, width), lambda i: (i, 0))
    return pl.pallas_call(
        query_kernel,
        grid=(length // tile,),
        in_specs=[rows, full((1, width)), full((1, width)), full(weight.shape), full((1, width))],
        out_specs=[rows, rows],
        out_shape=[jax.ShapeDtypeStruct(x.shape, bf16)] * 2,
        compiler_params=params(),
        cost_estimate=cost(2 * length * width * width, 6 * length * width + 2 * width * width),
        name="query",
    )(x, gain, shift, weight, bias)


def pair_kernel(me_ref, x_ref, rows_ref, *rest, count):
    pieces, (n_ref, k_ref, v_ref, w_ref) = rest[:count], rest[-4:]
    if count == 4:

        @pl.when(pl.program_id(0) == 0)
        def _():
            low = me_ref[0] & 3
            for place in range(4):
                w_ref[place ^ low] = pieces[place][...]

        weights = w_ref
    else:
        weights = pieces[0]
    half = weights.shape[1]
    norm, _ = normal_rows(x_ref[...].astype(f32))
    low = (norm * rows_ref[0:1, :] + rows_ref[1:2, :]).astype(bf16)
    n_ref[...] = low
    left, right = low[:, :half], low[:, half:]
    k_ref[...] = (nn(left, weights[0]) + nn(right, weights[1])).astype(bf16)
    v_ref[...] = (nn(left, weights[2]) + nn(right, weights[3]) + rows_ref[2:3, :]).astype(bf16)


def pair_call(page, length, me, x, rows, pieces, before):
    page_len, width = x.shape
    tile = 256
    first = page * page_len // tile
    placed = pl.BlockSpec((tile, width), lambda i, *_: (i + first, 0))
    left = pl.BlockSpec(memory_space=pl.ANY)
    weights = (4, width // 2, width)
    out_specs = [placed] * 3
    shapes = [jax.ShapeDtypeStruct((length, width), bf16)] * 3
    scratch = []
    if len(pieces) == 4:
        out_specs = out_specs + [full(weights)]
        shapes = shapes + [jax.ShapeDtypeStruct(weights, bf16)]
    else:
        scratch = [pltpu.VMEM((8, 128), f32)]
    grid_spec = pltpu.PrefetchScalarGridSpec(
        num_scalar_prefetch=1,
        grid=(page_len // tile,),
        in_specs=[
            pl.BlockSpec((tile, width), lambda i, *_: (i, 0)),
            full(rows.shape),
        ]
        + [full(piece.shape) for piece in pieces]
        + [left] * len(before),
        out_specs=out_specs,
        scratch_shapes=scratch,
    )
    return pl.pallas_call(
        functools.partial(pair_kernel, count=len(pieces)),
        grid_spec=grid_spec,
        out_shape=shapes,
        input_output_aliases={3 + len(pieces) + i: i for i in range(len(before))},
        compiler_params=params(),
        cost_estimate=cost(4 * page_len * width * width, 8 * page_len * width),
        name="pair",
    )(me, x, rows, *pieces, *before)


def head_lanes(value, head, head_dim):
    lane = lax.broadcasted_iota(jnp.int32, value.shape, 1)
    mine = (lane >= head * head_dim) & (lane < (head + 1) * head_dim)
    return jnp.where(mine, value, jnp.zeros_like(value))


def attend_kernel(q_ref, k_ref, v_ref, bias_ref, hq_ref, hk_ref, *rest):
    o_ref, lse_ref = rest[-2:]
    q, v = q_ref[...], v_ref[...]
    left = jnp.concatenate([k_ref[...], hk_ref[0]], 1)
    v_turned = v.astype(f32).T.astype(bf16)
    parts = []
    for head in range(2):
        picked = nn(hq_ref[0], bias_ref[0, head]).astype(bf16)
        right = jnp.concatenate([head_lanes(q, head, 64), picked], 1)
        scores = nt(left, right)
        peak = jnp.max(scores, 0, keepdims=True)
        raised = jnp.exp(scores - peak)
        total = jnp.sum(raised, 0, keepdims=True)
        probs = (raised * (1.0 / total)).astype(bf16)
        parts.append(nn(v_turned[head * 64 : (head + 1) * 64], probs))
        lse_ref[0, 0, head : head + 1, :] = peak + jnp.log(total)
    o_ref[...] = jnp.concatenate(parts, 0).T.astype(bf16)


def attend_specs(page_len, page, pair):
    rows = pl.BlockSpec((page_len, 128), lambda p, h: (p + page, h + pair))
    bias = pl.BlockSpec((1, 2, 64, 128), lambda p, h: (p + page, h + pair, 0, 0))
    lse = pl.BlockSpec((1, 1, 2, page_len), lambda p, h: (p + page, h + pair, 0, 0))

    def hot(*shape):
        return pl.BlockSpec((1,) + shape, lambda p, h: (p + page, 0, 0))

    return rows, bias, lse, hot


def attend_call(page, q, k, v, bias, hot_q, hot_k, before):
    length, width = q.shape
    pages, page_len = hot_q.shape[0], hot_q.shape[1]
    rows, bias_spec, lse, hot = attend_specs(page_len, page, 0)
    left = pl.BlockSpec(memory_space=pl.ANY)
    return pl.pallas_call(
        attend_kernel,
        grid=(1, width // 128),
        in_specs=[rows, rows, rows, bias_spec, hot(page_len, 64), hot(page_len, 128)]
        + [left] * len(before),
        out_specs=[rows, lse],
        out_shape=[
            jax.ShapeDtypeStruct((length, width), bf16),
            jax.ShapeDtypeStruct((pages, width // 128, 2, page_len), f32),
        ],
        input_output_aliases={6 + i: i for i in range(len(before))},
        compiler_params=params(),
        cost_estimate=cost(
            16 * page_len * page_len * width,
            8 * page_len * width,
            page_len * page_len * HEADS,
        ),
        name="attend",
    )(q, k, v, bias, hot_q, hot_k, *before)


def attend_back_kernel(
    q_ref,
    k_ref,
    v_ref,
    bias_ref,
    hq_ref,
    hk_ref,
    hkt_ref,
    lse_ref,
    o_ref,
    do_ref,
    dq_ref,
    dk_ref,
    dv_ref,
    gb_ref,
):
    q, k, v, do = q_ref[...], k_ref[...], v_ref[...], do_ref[...]
    hot_q = hq_ref[0]
    left = jnp.concatenate([k, hk_ref[0]], 1)
    k_turned = k.astype(f32).T.astype(bf16)
    overlap = do.astype(f32) * o_ref[...].astype(f32)
    row = lax.broadcasted_iota(jnp.int32, (8, 128), 0)
    lane = lax.broadcasted_iota(jnp.int32, (8, 128), 1)
    chooser = (row == lane // 64).astype(f32)
    delta = lax.dot_general(
        chooser,
        overlap,
        (((1,), (1,)), ((), ())),
        preferred_element_type=f32,
        precision=precise_variant,
    )
    parts, dk, dv = [], 0.0, 0.0
    for head in range(2):
        q_head, do_head = head_lanes(q, head, 64), head_lanes(do, head, 64)
        picked = nn(hot_q, bias_ref[0, head]).astype(bf16)
        right = jnp.concatenate([q_head, picked], 1)
        probs = jnp.exp(nt(left, right) - lse_ref[0, 0, head : head + 1, :])
        slope = nt(v, do_head)
        turn = (probs * (slope - delta[head : head + 1, :])).astype(bf16)
        dv = dv + nn(probs.astype(bf16), do_head)
        dk = dk + nn(turn, q_head)
        both = nn(jnp.concatenate([k_turned[head * 64 : (head + 1) * 64], hkt_ref[0]], 0), turn)
        parts.append(both[:64])
        sums = both[64:]
        high = sums.astype(bf16)
        rest = (sums - high.astype(f32)).astype(bf16)
        gb_ref[0, head] = nn(high, hot_q) + nn(rest, hot_q)
    dq_ref[...] = (jnp.concatenate(parts, 0) * score_scale).T.astype(bf16)
    dk_ref[...] = dk.astype(bf16)
    dv_ref[...] = dv.astype(bf16)


def attend_back_call(group, groups, q, k, v, bias, hot_q, hot_k, hot_kt, lse_in, o, do):
    length, width = q.shape
    pages, page_len = hot_q.shape[0], hot_q.shape[1]
    pairs = width // 128 // groups
    rows, bias_spec, lse, hot = attend_specs(page_len, 0, group * pairs)
    given = pl.BlockSpec((page_len, 128), lambda p, h: (p, h))
    grad_bias = pl.BlockSpec((1, 2, 64, 64), lambda p, h: (p, h, 0, 0))
    wide = jax.ShapeDtypeStruct((length, width // groups), bf16)
    return pl.pallas_call(
        attend_back_kernel,
        grid=(pages, pairs),
        in_specs=[
            rows,
            rows,
            rows,
            bias_spec,
            hot(page_len, 64),
            hot(page_len, 128),
            hot(64, page_len),
            lse,
            rows,
            rows,
        ],
        out_specs=[given, given, given, grad_bias],
        out_shape=[
            wide,
            wide,
            wide,
            jax.ShapeDtypeStruct((pages, HEADS // groups, 64, 64), f32),
        ],
        compiler_params=params(),
        cost_estimate=cost(
            40 * length * page_len * width // groups,
            16 * length * width // groups,
            length * page_len * HEADS // groups,
        ),
        name="attend_back",
    )(q, k, v, bias, hot_q, hot_k, hot_kt, lse_in, o, do)


def put_rows(scratch, keep, send, at, me, relative):
    if not relative:
        keep[pl.ds(at, scratch.shape[0]), :] = scratch[...].astype(bf16)
        return
    step = scratch.shape[0] // 16
    for place in range(16):
        owner = place ^ me
        rows = scratch[pl.ds(pl.multiple_of(owner * step, step), step), :].astype(bf16)
        target = send if place & 1 else keep
        low = at + (place >> 2) * step
        target[(place >> 1) & 1, low : low + step, :] = rows


def put_quarter(scratch, keep, send, at, me, relative):
    if not relative:
        keep[pl.ds(at, scratch.shape[0]), :] = scratch[...].astype(bf16)
        return
    step = scratch.shape[0] // 4
    for place in range(4):
        owner = place ^ (me & 3)
        rows = scratch[pl.ds(pl.multiple_of(owner * step, step), step), :].astype(bf16)
        target = send if place & 1 else keep
        target[place >> 1, at : at + step, :] = rows


def block_shapes(rows, width, relative):
    if relative:
        return (2, rows // 4, width), (2, rows // 4, width)
    return (rows, width), (16, 128)


def middle_kernel(
    x_ref, mixed_ref, keep_ref, wo_ref, bo_ref, gain_ref, shift_ref, middle_ref, n2_ref, small_ref
):
    @pl.when(pl.program_id(0) == 0)
    def _():
        small_ref[...] = jnp.zeros_like(small_ref)

    branch = nn(mixed_ref[...], wo_ref[...]) + bo_ref[...]
    middle = x_ref[...].astype(f32) + branch
    middle_ref[...] = middle
    norm, _ = normal_rows(middle)
    n2_ref[...] = (norm * gain_ref[...] + shift_ref[...]).astype(bf16)
    small_ref[15:16, :] += jnp.sum(branch * branch * keep_ref[...], 0, keepdims=True)
    small_ref[17:18, :] += jnp.broadcast_to(
        jnp.sum(keep_ref[...], 0, keepdims=True), (1, small_ref.shape[1])
    )


def middle_call(x, mixed, keep, wo, bo, gain, shift):
    length, width = x.shape
    tile = 256
    rows = pl.BlockSpec((tile, width), lambda i: (i, 0))
    row = full((1, width))
    shape = jax.ShapeDtypeStruct
    return pl.pallas_call(
        middle_kernel,
        grid=(length // tile,),
        in_specs=[
            rows,
            rows,
            pl.BlockSpec((tile, 1), lambda i: (i, 0)),
            full((width, width)),
            row,
            row,
            row,
        ],
        out_specs=[rows, rows, full((SMALL, width))],
        out_shape=[
            shape((length, width), f32),
            shape((length, width), bf16),
            shape((SMALL, width), f32),
        ],
        compiler_params=params(),
        cost_estimate=cost(4 * length * width * width, 10 * length * width),
        name="middle",
    )(x, mixed, keep, wo, bo, gain, shift)


def feed_kernel(
    me_ref,
    n2_ref,
    cot_ref,
    cots_ref,
    n2s_ref,
    up_ref,
    upb_ref,
    down_ref,
    old_ref,
    *rest,
    block,
    relative,
    tile,
):
    before, rest = rest[:-8], rest[-8:]
    feed_ref, gn_ref, small_ref, kept_ref, sent_ref, act_ref, gh_ref, dw_ref = rest
    step = pl.program_id(0)
    up, down = up_ref[...], down_ref[...]

    @pl.when(step == 0)
    def _():
        small_ref[...] = old_ref[...]

    at = pl.ds(pl.multiple_of(step * tile, tile), tile)
    hidden = nn(n2_ref[...], up) + upb_ref[...]
    gate = 0.5 * (1.0 + lax.erf(hidden * 0.7071067811865476))
    bell = jnp.exp(hidden * hidden * -0.5) * 0.3989422804014327
    act = (hidden * gate).astype(bf16)
    act_ref[at, :] = act
    gh = (nt(cot_ref[...], down) * (gate + hidden * bell)).astype(bf16)
    gh_ref[at, :] = gh
    small_ref[10 + block : 11 + block, :] += jnp.sum(gh.astype(f32), 0, keepdims=True)
    feed, gn = nn(act, down), nt(gh, up)
    if before:
        feed, gn = feed + before[0][...], gn + before[1][...]
    feed_ref[...] = feed
    gn_ref[...] = gn

    @pl.when(step == pl.num_programs(0) - 1)
    def _():
        me = me_ref[0]
        dw_ref[...] = tn(n2s_ref[...], gh_ref[...])
        put_rows(dw_ref, kept_ref, sent_ref, 0, me, relative)
        dw_ref[...] = tn(act_ref[...], cots_ref[...])
        put_quarter(dw_ref, kept_ref, sent_ref, 192 if relative else 768, me, relative)


def feed_call(block, me, n2, cot, up, upb, down, small, before, relative):
    length, width = n2.shape
    tile = 256
    rows = pl.BlockSpec((tile, width), lambda i, *_: (i, 0))
    whole = full((length, width))
    kept, sent = block_shapes(2 * width, width, relative)
    shape = jax.ShapeDtypeStruct
    grid_spec = pltpu.PrefetchScalarGridSpec(
        num_scalar_prefetch=1,
        grid=(length // tile,),
        in_specs=[
            rows,
            rows,
            whole,
            whole,
            pl.BlockSpec((width, width), lambda i, *_: (0, block)),
            pl.BlockSpec((1, width), lambda i, *_: (0, block)),
            pl.BlockSpec((width, width), lambda i, *_: (block, 0)),
            full((SMALL, width)),
        ]
        + [rows] * len(before),
        out_specs=[rows, rows, full((SMALL, width)), full(kept), full(sent)],
        scratch_shapes=[
            pltpu.VMEM((length, width), bf16),
            pltpu.VMEM((length, width), bf16),
            pltpu.VMEM((width, width), f32),
        ],
    )
    return pl.pallas_call(
        functools.partial(feed_kernel, block=block, relative=relative, tile=tile),
        grid_spec=grid_spec,
        out_shape=[
            shape((length, width), f32),
            shape((length, width), f32),
            shape((SMALL, width), f32),
            shape(kept, bf16),
            shape(sent, bf16),
        ],
        input_output_aliases={9 + i: i for i in range(len(before))},
        compiler_params=params(),
        cost_estimate=cost(
            12 * length * width * width, 20 * length * width, 2 * length * width
        ),
        name="feed",
    )(me, n2, cot, cot, n2, up, upb, down, small, *before)


def finish_kernel(
    me_ref,
    feed_ref,
    gn_ref,
    middle_ref,
    cot_ref,
    keep_ref,
    mixed_ref,
    wo_ref,
    gain_ref,
    downb_ref,
    old_ref,
    out_ref,
    gm_ref,
    gx_ref,
    small_ref,
    kept_ref,
    sent_ref,
    low_ref,
    dw_ref,
    *,
    relative,
    tile,
):
    step = pl.program_id(0)

    @pl.when(step == 0)
    def _():
        small_ref[...] = old_ref[...]

    at = pl.ds(pl.multiple_of(step * tile, tile), tile)
    feed = feed_ref[...] + downb_ref[...]
    middle = middle_ref[...]
    output = middle + feed
    out_ref[...] = output.astype(bf16)
    weight = keep_ref[...]
    cot = cot_ref[...].astype(f32)
    norm, scale = normal_rows(middle)
    grad = gn_ref[...]
    inner = grad * gain_ref[...]
    grad_middle = cot + scale * (
        inner
        - jnp.mean(inner, -1, keepdims=True)
        - norm * jnp.mean(inner * norm, -1, keepdims=True)
    )
    gm_ref[...] = grad_middle
    low = grad_middle.astype(bf16)
    low_ref[at, :] = low
    gx_ref[...] = nt(low, wo_ref[...]).astype(bf16)
    small_ref[0:1, :] += jnp.sum(low.astype(f32), 0, keepdims=True)
    small_ref[1:2, :] += jnp.sum(grad * norm, 0, keepdims=True)
    small_ref[2:3, :] += jnp.sum(grad, 0, keepdims=True)
    small_ref[3:4, :] += jnp.sum(cot, 0, keepdims=True)
    small_ref[14:15, :] += jnp.sum(output * output * weight, 0, keepdims=True)
    small_ref[16:17, :] += jnp.sum(feed * feed * weight, 0, keepdims=True)

    @pl.when(step == pl.num_programs(0) - 1)
    def _():
        dw_ref[...] = tn(mixed_ref[...], low_ref[...])
        put_rows(dw_ref, kept_ref, sent_ref, 0, me_ref[0], relative)


def finish_call(me, feed, gn, middle, cot, keep, mixed, wo, gain, downb, small, relative):
    length, width = mixed.shape
    tile = 256
    rows = pl.BlockSpec((tile, width), lambda i, *_: (i, 0))
    row = full((1, width))
    kept, sent = block_shapes(width, width, relative)
    shape = jax.ShapeDtypeStruct
    grid_spec = pltpu.PrefetchScalarGridSpec(
        num_scalar_prefetch=1,
        grid=(length // tile,),
        in_specs=[
            rows,
            rows,
            rows,
            rows,
            pl.BlockSpec((tile, 1), lambda i, *_: (i, 0)),
            full((length, width)),
            full((width, width)),
            row,
            row,
            full((SMALL, width)),
        ],
        out_specs=[rows, rows, rows, full((SMALL, width)), full(kept), full(sent)],
        scratch_shapes=[pltpu.VMEM((length, width), bf16), pltpu.VMEM((width, width), f32)],
    )
    return pl.pallas_call(
        functools.partial(finish_kernel, relative=relative, tile=tile),
        grid_spec=grid_spec,
        out_shape=[
            shape((length, width), bf16),
            shape((length, width), f32),
            shape((length, width), bf16),
            shape((SMALL, width), f32),
            shape(kept, bf16),
            shape(sent, bf16),
        ],
        compiler_params=params(),
        cost_estimate=cost(4 * length * width * width, 24 * length * width),
        name="finish",
    )(me, feed, gn, middle, cot, keep, mixed, wo, gain, downb, small)


def weights_kernel(
    me_ref,
    x_ref,
    xp_ref,
    n_ref,
    np_ref,
    dq_ref,
    dk_ref,
    dv_ref,
    wq_ref,
    wp_ref,
    old_ref,
    *rest,
    group,
    relative,
    tile,
    last,
):
    before, rest = rest[:-6], rest[-6:]
    gq_ref, gp_ref, small_ref, kept_ref, sent_ref, dw_ref = rest
    me = me_ref[0]
    length, width = x_ref.shape
    part = dq_ref.shape[1]
    lanes = slice(group * part, (group + 1) * part)
    small_ref[...] = old_ref[...]
    wk = wp_ref[0:2].reshape(width, part)
    wv = wp_ref[2:4].reshape(width, part)

    @pl.loop(0, length // tile)
    def _(i):
        at = pl.ds(pl.multiple_of(i * tile, tile), tile)
        dq, dk, dv = dq_ref[at, :], dk_ref[at, :], dv_ref[at, :]
        far = nt(dk, wk) + nt(dv, wv)
        own = nt(dq, wq_ref[...])
        if before:
            own, far = own + before[0][at, :], far + before[1][at, :]
        gq_ref[at, :] = own
        gp_ref[at, :] = far.astype(gp_ref.dtype)
        small_ref[4:5, lanes] += jnp.sum(dq.astype(f32), 0, keepdims=True)
        small_ref[7:8, lanes] += jnp.sum(dv.astype(f32), 0, keepdims=True)
        if last:
            norm, _ = normal_rows(x_ref[at, :].astype(f32))
            far_norm, _ = normal_rows(xp_ref[at, :].astype(f32))
            small_ref[5:6, :] += jnp.sum(own * norm, 0, keepdims=True)
            small_ref[6:7, :] += jnp.sum(own, 0, keepdims=True)
            small_ref[8:9, :] += jnp.sum(far * far_norm, 0, keepdims=True)
            small_ref[9:10, :] += jnp.sum(far, 0, keepdims=True)

    step = 192 if relative else 768
    dw_ref[...] = tn(n_ref[...], dq_ref[...])
    put_rows(dw_ref, kept_ref, sent_ref, 0, me, relative)
    dw_ref[...] = tn(np_ref[...], dk_ref[...])
    put_rows(dw_ref, kept_ref, sent_ref, step, me, relative)
    dw_ref[...] = tn(np_ref[...], dv_ref[...])
    put_rows(dw_ref, kept_ref, sent_ref, 2 * step, me, relative)


def weights_call(group, groups, me, x, xp, n, n_far, dq, dk, dv, wq, wp, small, before, relative):
    length, width = x.shape
    part = width // groups
    last = group == groups - 1
    rows, some = full((length, width)), full((length, part))
    columns = pl.BlockSpec((width, part), lambda i, *_: (0, group))
    far_columns = pl.BlockSpec((4, width // 2, part), lambda i, *_: (0, 0, group))
    kept, sent = block_shapes(3 * width, part, relative)
    shape = jax.ShapeDtypeStruct
    grid_spec = pltpu.PrefetchScalarGridSpec(
        num_scalar_prefetch=1,
        grid=(1,),
        in_specs=[rows] * 4
        + [some] * 3
        + [columns, far_columns, full((SMALL, width))]
        + [rows] * len(before),
        out_specs=[rows, rows, full((SMALL, width)), full(kept), full(sent)],
        scratch_shapes=[pltpu.VMEM((width, part), f32)],
    )
    return pl.pallas_call(
        functools.partial(
            weights_kernel, group=group, relative=relative, tile=256, last=last
        ),
        grid_spec=grid_spec,
        out_shape=[
            shape((length, width), f32),
            shape((length, width), bf16 if last else f32),
            shape((SMALL, width), f32),
            shape(kept, bf16),
            shape(sent, bf16),
        ],
        compiler_params=params(),
        cost_estimate=cost(12 * length * width * part, 24 * length * width),
        name="weights",
    )(me, x, xp, n, n_far, dq, dk, dv, wq, wp, small, *before)


def tokens_kernel(x_ref, gain_ref, gm_ref, gq_ref, gf_ref, out_ref):
    norm, scale = normal_rows(x_ref[...].astype(f32))
    inner = (gq_ref[...] + gf_ref[...].astype(f32)) * gain_ref[...]
    out_ref[...] = gm_ref[...] + scale * (
        inner
        - jnp.mean(inner, -1, keepdims=True)
        - norm * jnp.mean(inner * norm, -1, keepdims=True)
    )


def tokens_call(x, gain, gm, gq, gf):
    length, width = x.shape
    rows = pl.BlockSpec((256, width), lambda i: (i, 0))
    return pl.pallas_call(
        tokens_kernel,
        grid=(length // 256,),
        in_specs=[rows, full((1, width)), rows, rows, rows],
        out_specs=rows,
        out_shape=jax.ShapeDtypeStruct((length, width), f32),
        compiler_params=params(),
        cost_estimate=cost(20 * length * width, 16 * length * width),
        name="tokens",
    )(x, gain, gm, gq, gf)


def swapped(value, axis, mask):
    pairs = [(source, source ^ mask) for source in range(lax.axis_size(axis))]
    return lax.ppermute(value, axis, pairs)


def added(a, b, dtype=bf16):
    return (a.astype(f32) + b.astype(f32)).astype(dtype)


def together(kernel, inputs, moves):
    inputs, values = lax.optimization_barrier((inputs, [value for value, _, _ in moves]))
    came = [swapped(value, *way[1:]) for value, way in zip(values, moves)]
    results = kernel(*inputs) if kernel else []
    return lax.optimization_barrier((results, came))


def core_add(pair, came):
    return added(pair[0][0], came[0]), added(pair[0][1], came[1])


def z_parts(value):
    return value[0::2], value[1::2]


def everywhere(value):
    mask = 1
    while mask < lax.axis_size("dp"):
        value = value + swapped(value, "dp", mask)
        mask *= 2
    return value


def pick_stream(pair, stream):
    return jnp.where(stream == 0, pair[0], pair[1])


def box_onehots(seg_boxes, buckets):
    half = buckets // 2
    levels = jnp.arange(buckets, dtype=jnp.int32)
    centre_x = (seg_boxes[..., 0] + seg_boxes[..., 2]) // 2
    centre_y = (seg_boxes[..., 1] + seg_boxes[..., 3]) // 2
    step_x = (
        jnp.clip((centre_x[:, None, :] - centre_x[:, :, None]) // box_step, -half, half - 1) + half
    )
    step_y = (
        jnp.clip((centre_y[:, None, :] - centre_y[:, :, None]) // box_step, -half, half - 1) + half
    )
    return (
        (step_x[..., None] == levels).astype(jnp.float32),
        (step_y[..., None] == levels).astype(jnp.float32),
    )


def body(
    tokens,
    first_gain,
    first_shift,
    query_weight,
    query_bias,
    key_weight,
    value_weight,
    value_bias,
    out_weight,
    out_bias,
    second_gain,
    second_shift,
    up_weight,
    up_bias,
    down_weight,
    down_bias,
    box_table,
    segments,
    validity,
    seg_boxes,
    cotangent,
):
    stream = lax.axis_index("stream")
    me = lax.axis_index("dp")
    shards = lax.axis_size("dp")
    width = tokens.shape[2]
    hidden = up_weight.shape[2]
    pages, page_len = segments.shape[1], segments.shape[2]
    length = pages * page_len
    relative = shards == 16
    me_ref = me.reshape(1).astype(jnp.int32)
    x = tokens[0]

    own_seg = pick_stream(segments, stream)
    far_seg = pick_stream(segments, 1 - stream)
    own_keep = pick_stream(validity, stream)
    far_keep = pick_stream(validity, 1 - stream)
    levels = jnp.arange(64, dtype=jnp.int32)
    hot_q = (own_seg[:, :, None] == levels).astype(bf16)
    hot_kt = (far_seg[:, None, :] == levels[None, :, None]).astype(bf16)
    wide_levels = jnp.arange(128, dtype=jnp.int32)
    hot_k = jnp.where(
        wide_levels == 64,
        jnp.where(far_keep[:, :, None] > 0, 0.0, mask_fill),
        (far_seg[:, :, None] == wide_levels).astype(f32),
    ).astype(bf16)
    hot_x, hot_y = box_onehots(seg_boxes, BUCKETS)
    tables = box_table[0].reshape(2, HEADS, BUCKETS)
    seg_bias = (
        jnp.einsum("pabn,hn->phab", hot_x, tables[0], precision=precise_variant)
        + jnp.einsum("pabn,hn->phab", hot_y, tables[1], precision=precise_variant)
    ).astype(bf16)
    ones = (jnp.arange(64) == 0).astype(bf16)
    seg_bias = jnp.concatenate([seg_bias, jnp.broadcast_to(ones, seg_bias.shape)], -1)

    keep_column = own_keep.reshape(length, 1).astype(f32)
    blocks, groups = hidden // width, 2
    part, chunk = width // groups, width // shards
    cot = cotangent[0]
    Y, CORE, X, Z1, Z2 = ("stream", 1), ("dp", 1), ("dp", 2), ("dp", 4), ("dp", 8)

    low = me & 3
    half = width // 2

    def quarter(weight):
        return lax.dynamic_slice_in_dim(weight[0], (low & 1) * half, half, 0)

    piece = jnp.where(low < 2, quarter(key_weight), quarter(value_weight))
    vectors = jnp.concatenate([first_gain, first_shift, value_bias], 0)
    (normed, query), (piece, far_rows) = together(
        query_call,
        (x, first_gain, first_shift, query_weight[0], query_bias),
        [(piece, *Y), (vectors, *Y)],
    )
    page_x = [x[page * page_len : (page + 1) * page_len] for page in range(pages)]
    (seg_bias, hot_q, hot_k), (x_piece, core_piece, came_x) = together(
        lambda *same: same,
        (seg_bias, hot_q, hot_k),
        [(piece, *X), (piece, *CORE), (page_x[0], *Y)],
    )
    far_pages = [came_x]
    pieces = [piece, core_piece, x_piece, swapped(x_piece, *CORE)]
    far, mixing = (), ()
    for page in range(pages):

        def page_step(came, pieces, far, mixing, page=page):
            far = pair_call(page, length, me_ref, came, far_rows, pieces, far)
            return far, attend_call(page, query, far[1], far[2], seg_bias, hot_q, hot_k, mixing)

        moves = [(page_x[page + 1], *Y)] if page + 1 < pages else []
        (result, mixing), came = together(
            page_step, (far_pages[page], pieces, tuple(far), tuple(mixing)), moves
        )
        far, mixing = result[:3], mixing
        if page == 0:
            pieces = [result[3]]
        far_pages += came
    far_normed, keys, value_rows = far
    far_weights = pieces[0]
    mixed, log_total = mixing

    middle, normed_two, small = middle_call(
        x, mixed, keep_column, out_weight[0], out_bias, second_gain, second_shift
    )

    def feed_block(block):
        def call(n2, small, *sums):
            return feed_call(
                block, me_ref, n2, cot, up_weight[0], up_bias, down_weight[0], small, sums, relative
            )

        return call

    def finish(feed, gn, small):
        return finish_call(
            me_ref, feed, gn, middle, cot, keep_column, mixed, out_weight[0], second_gain,
            down_bias, small, relative,
        )

    def back_group(group):
        def call(grad_mixed):
            return attend_back_call(
                group, groups, query, keys, value_rows, seg_bias, hot_q, hot_k, hot_kt, log_total,
                mixed, grad_mixed,
            )

        return call

    far_x = jnp.concatenate(far_pages, 0)

    def weights_group(group):
        def call(small, dq, dk, dv, *before):
            return weights_call(
                group, groups, me_ref, x, far_x, normed, far_normed, dq, dk, dv,
                query_weight[0], far_weights, small, before, relative,
            )

        return call

    def table_rows(small, grad_bias):
        grad_table = jnp.concatenate(
            [
                jnp.einsum("pabn,phba->hn", hot_x, grad_bias, precision=precise_variant),
                jnp.einsum("pabn,phba->hn", hot_y, grad_bias, precision=precise_variant),
            ],
            0,
        ).reshape(1, -1)
        return small + jnp.pad(grad_table, ((18, SMALL - 19), (0, 0)))

    if relative:
        (*sums, small, k0, s0), _ = together(feed_block(0), (normed_two, small), [])
        (*sums, small, k1, s1), (c0,) = together(
            feed_block(1), (normed_two, small, *sums), [(s0, *CORE)]
        )
        m0, t0 = core_add((k0,), c0)
        (*sums, small, k2, s2), (c1, x0) = together(
            feed_block(2), (normed_two, small, *sums), [(s1, *CORE), (t0, *X)]
        )
        n0 = added(m0, x0)
        m1, t1 = core_add((k1,), c1)
        (*sums, small, k3, s3), (c2, x1) = together(
            feed_block(3), (normed_two, small, *sums), [(s2, *CORE), (t1, *X)]
        )
        n1 = added(m1, x1)
        m2, t2 = core_add((k2,), c2)

        def quads(*values):
            return jnp.concatenate([value.reshape(4, 48, -1) for value in values], 1)

        up_keep, up_go = z_parts(quads(n0[:192], n1[:192]))
        (output, grad_middle, grad_mixed, small, ko, so), (c3, x2, z0) = together(
            finish, (*sums, small), [(s3, *CORE), (t2, *X), (up_go, *Z1)]
        )
        n2 = added(m2, x2)
        m3, t3 = core_add((k3,), c3)
        up_half = added(up_keep, z0)
        (dq, dk, dv, grad_bias), (co, x3, z0) = together(
            back_group(0), (grad_mixed,), [(so, *CORE), (t3, *X), (up_half[1], *Z2)]
        )
        up_low = added(up_half[0], z0, f32)
        n3 = added(m3, x3)
        mo, to = core_add((ko,), co)
        down = jnp.stack([value[192:] for value in (n0, n1, n2, n3)])
        down_keep, down_go = z_parts(down[jnp.arange(4) ^ (me >> 2)])
        (*sums, small, kq, sq), (xo, z0) = together(
            weights_group(0), (small, dq, dk, dv), [(to, *X), (down_go, *Z1)]
        )
        no = added(mo, xo)
        down_half = added(down_keep, z0)
        rest_keep, rest_go = z_parts(quads(n2[:192], n3[:192], no))
        (dq, dk, dv, grad_bias_two), (cq, z0, z1) = together(
            back_group(1),
            (grad_mixed,),
            [(sq, *CORE), (down_half[1], *Z2), (rest_go, *Z1)],
        )
        sum_down = added(down_half[0], z0, f32)
        rest_half = added(rest_keep, z1)
        mq, tq = core_add((kq,), cq)
        (own_grad, far_grad, small, kr, sr), (xq, z0) = together(
            weights_group(1), (small, dq, dk, dv, *sums), [(tq, *X), (rest_half[1], *Z2)]
        )
        rest = added(rest_half[0], z0, f32)
        sum_up = jnp.concatenate([up_low[:48], up_low[48:], rest[:48], rest[48:96]], 1)
        sum_out = rest[96:]
        small = table_rows(small, jnp.concatenate([grad_bias, grad_bias_two], 1))
        came_grad = swapped(far_grad, *Y)
        nq = added(mq, xq)
        q_keep, q_go = z_parts(quads(nq[:192], nq[192:384], nq[384:]))
        _, (cr, z0, came) = together(None, (), [(sr, *CORE), (q_go, *Z1), (small, *CORE)])
        small = small + came
        mr, tr = core_add((kr,), cr)
        q_half = added(q_keep, z0)
        _, (xr, z0, came) = together(None, (), [(tr, *X), (q_half[1], *Z2), (small, *X)])
        small = small + came
        first = added(q_half[0], z0, f32)
        nr = added(mr, xr)
        r_keep, r_go = z_parts(quads(nr[:192], nr[192:384], nr[384:]))
        _, (z0, came) = together(None, (), [(r_go, *Z1), (small, *Z1)])
        small = small + came
        r_half = added(r_keep, z0)
        _, (z0, came) = together(None, (), [(r_half[1], *Z2), (small, *Z2)])
        small = small + came
        second = added(r_half[0], z0, f32)
        three = jnp.concatenate([first, second], 1)
        sum_query, sum_pair = three[:48], three[48:].astype(bf16)
    else:
        sums, grads = (), []
        for block in range(blocks):
            *sums, small, kept, sent = feed_block(block)(normed_two, small, *sums)
            grads.append(kept)
        output, grad_middle, grad_mixed, small, out_kept, _ = finish(*sums, small)
        back_sums, grad_biases, parts = (), [], []
        for group in range(groups):
            dq, dk, dv, grad_bias = back_group(group)(grad_mixed)
            *back_sums, small, kept, _ = weights_group(group)(small, dq, dk, dv, *back_sums)
            grad_biases.append(grad_bias)
            parts.append(kept)
        own_grad, far_grad = back_sums
        came_grad = swapped(far_grad, *Y)
        small = everywhere(table_rows(small, jnp.concatenate(grad_biases, 1)))

        def scattered(value):
            return lax.psum_scatter(value.astype(f32), "dp", scatter_dimension=0, tiled=True)

        sum_up = scattered(jnp.concatenate([kept[:width] for kept in grads], 1))
        sum_down = scattered(jnp.concatenate([kept[width:] for kept in grads], 0))
        sum_out = scattered(out_kept)
        three = jnp.concatenate(parts, 1)
        sum_query = scattered(three[:width])
        sum_pair = jnp.concatenate(
            [scattered(three[width : 2 * width]), scattered(three[2 * width :])], 0
        ).astype(bf16)

    lanes = lax.dynamic_slice_in_dim(small, me * chunk, chunk, 1)
    grad_tokens = tokens_call(x, first_gain, grad_middle, own_grad, came_grad)
    sum_pair, back = swapped((sum_pair, lanes[7:10]), *Y)
    sum_keys, sum_values = sum_pair[:chunk].astype(f32), sum_pair[chunk:].astype(f32)
    up_part = lax.dynamic_slice_in_dim(
        small[10 : 10 + blocks].reshape(1, hidden), me * (hidden // shards), hidden // shards, 1
    )
    totals = jnp.sum(small[14:17], 1)
    root_means = jnp.sqrt(totals / (small[17, 0] * width) + 1e-06).reshape(1, 3)

    return (
        output[None],
        grad_tokens[None],
        lanes[5:6] + back[1:2],
        lanes[6:7] + back[2:3],
        sum_query[None],
        lanes[4:5],
        sum_keys[None],
        sum_values[None],
        back[0:1],
        sum_out[None],
        lanes[0:1],
        lanes[1:2],
        lanes[2:3],
        sum_up[None],
        up_part,
        sum_down[None],
        lanes[3:4],
        lanes[18:19],
        root_means,
    )


def solution(mesh):
    whole, split = P("stream", None), P("stream", "dp")
    cube, cut = P("stream", None, None), P("stream", "dp", None)
    pages = P(None, "dp", None)
    in_specs = (
        cut, whole, whole, cube, whole, cube, cube, whole, cube, whole, whole, whole,
        cube, whole, cube, whole, whole, pages, pages, P("dp", None, None), cut,
    )
    out_specs = (
        cut, cut, split, split, cut, split, cut, cut, split, cut, split, split, split,
        cut, split, cut, split, split, whole,
    )
    return jax.shard_map(body, mesh=mesh, in_specs=in_specs, out_specs=out_specs, check_vma=False)
```

time: 398 us -> 339 us (0.85)
  waiting for transfers between devices: 160 us -> 54.1 us
  Pallas kernels: 141 us -> 187 us
  local copies, waits for them, and re-layouts: 34.2 us -> 20.9 us
  starting transfers between devices: 29.3 us -> 37.6 us
    ppermute x28 -> x38, waiting for transfers between devices: 160 us -> 54.1 us  [swapped(): return lax.ppermute(value, axis, pairs)]
    pallas_call x5 -> x14, Pallas kernels: 128 us -> 174 us  [the longest x4 62.4 us: feed_call(): pl.pallas_call(functools.partial(feed_kernel, block=block, relative=relat...]
    ppermute x28 -> x38, starting transfers between devices: 29.3 us -> 37.6 us  [swapped(): return lax.ppermute(value, axis, pairs)]
    convert_element_type x11 -> x19, other arithmetic: 8.99 us -> 15.6 us  [added(): return (a.astype(f32) + b.astype(f32)).astype(dtype)]
    squeeze x10 -> x5, local copies, waits for them, and re-layouts: 5.94 us -> 0.76 us  [the longest x1 0.7 us: body(): rest_half[1]]
    unnamed x41 -> x105, local copies, waits for them, and re-layouts: 8.05 us -> 12.6 us
    slice x13 -> x14, local copies, waits for them, and re-layouts: 8.91 us -> 4.68 us  [the longest x5 1.65 us: z_parts(): return (value[0::2], value[1::2])]
  transfers between devices with their start and end apart: 28 -> 38, of which waited for: 16 -> 12; matrix products, arithmetic and copies ran while one was open for 13% -> 5% of each run, Pallas kernels for 3% -> 45%
where the time goes in v2:
time: 339 us; the launch traced here: 334 us
  Pallas kernels  187 us (55%)
  waiting for transfers between devices  54.1 us (16%)
  starting transfers between devices  37.6 us (11%)
  other arithmetic  28.5 us (8%)
  local copies, waits for them, and re-layouts  20.9 us (6%)
  matrix products  4.06 us (1%)
    pallas_call x4, Pallas kernels, feed_call(): pl.pallas_call(functools.partial(feed_kernel, block=block, relative=relat...  62.4 us
    ppermute x38, waiting for transfers between devices, swapped(): return lax.ppermute(value, axis, pairs)  54.1 us
    ppermute x38, starting transfers between devices, swapped(): return lax.ppermute(value, axis, pairs)  37.6 us
    pallas_call x2, Pallas kernels, attend_back_call(): pl.pallas_call(attend_back_kernel, grid=(pages, pairs), in_specs=[rows, r...  33.1 us
    pallas_call x2, Pallas kernels, weights_call(): pl.pallas_call(functools.partial(weights_kernel, group=group, relative=re...  25.1 us
    pallas_call x2, Pallas kernels, attend_call(): pl.pallas_call(attend_kernel, grid=(1, width // 128), in_specs=[rows, row...  24.1 us
    convert_element_type x19, other arithmetic, added(): return (a.astype(f32) + b.astype(f32)).astype(dtype)  15.6 us
    unnamed x105, local copies, waits for them, and re-layouts  12.6 us
  transfers between devices with their start and end apart: 38, of which 12 were waited for; matrix products, arithmetic and copies ran while one was open for 5% of the time, Pallas kernels for 45%

profile of v2, /device:TPU:0, one launch (start us, length us, event | category | flops | bytes accessed | tf_op | source)
XLA Modules:
  0.0 334.5 jit_solution(1296279212026460628)
XLA Ops:
  1.4 1.4 select_bitcast_fusion
  2.8 3.0 collective-permute-start
  12.7 6.0 %query.1 = (bf16[1024,768]{1,0:T(8,128)(2,1)}, bf16[1024,768]{1,0:T(8,128)(2,1)}) custom-call(bf16[1024,768]{1,0:T(8,128)(2,1)} %bitcast.177, f32[1,768]{1,0:T(1,128)} %gain_ref.6, f32[1,768]{1,0:T(1,128)} %shift_ref.1, bf16[768,768]{1,0:T(8,128)(2,1)} %bitcast.196, f32[1,768]{1,0:T(1,128)} %b_ref), custom_call_target="tpu_custom_call" | custom-call | flops 1207959552 | bytes 5898240 | tf_op jit(solution)/shard_map/query/pallas_call | solution.py:68
  20.3 1.7 collective-permute-start.4
  22.0 1.5 collective-permute-start.2
  23.5 12.6 %collective-permute-done.2.rest_2_ = bf16[384,768]{1,0:T(8,128)(2,1)S(1)} collective-permute-done((bf16[384,768]{1,0:T(8,128)(2,1)}, bf16[384,768]{1,0:T(8,128)(2,1)S(1)}, u32[]{:S(2)}, u32[]{:S(2)}) %collective-permute-start.2) | collective-permute-done | bytes 589856 | tf_op jit(solution)/shard_map/ppermute | solution.py:693
  36.1 2.9 collective-permute-done.4.x_ref
  39.0 2.0 collective-permute-done.5.rest_3_
  41.8 1.4 collective-permute-start.6
  44.3 5.4 %pair.2 = (bf16[1024,768]{1,0:T(8,128)(2,1)}, bf16[1024,768]{1,0:T(8,128)(2,1)}, bf16[1024,768]{1,0:T(8,128)(2,1)}, bf16[4,384,768]{2,1,0:T(8,128)(2,1)}) custom-call(s32[1]{0:T(128)} %bitcast.me_ref, bf16[512,768]{1,0:T(8,128)(2,1)} %copy-done.22, f32[3,768]{1,0:T(4,128)} %copy-done.41, bf16[384,768]{1,0:T(8,128)(2,1)} %copy-done.46, ...), custom_call_target="tpu_custom_call" | custom-call | flops 1207959552 | bytes 3145728 | tf_op jit(solution)/shard_map/pair/pallas_call | solution.py:129
  49.7 12.1 %attend.2 = (bf16[1024,768]{1,0:T(8,128)(2,1)}, f32[2,6,2,512]{3,2,1,0:T(2,128)}) custom-call(bf16[1024,768]{1,0:T(8,128)(2,1)} %get-tuple-element.280.q_ref, bf16[1024,768]{1,0:T(8,128)(2,1)} %get-tuple-element.297.k_ref.rest_2_, bf16[1024,768]{1,0:T(8,128)(2,1)} %get-tuple-element.298.v_ref.rest_3_, bf16[2,12,64,128]{3,2,1,0:T(8,128)(2,1)} %pad_maximum_fusion.6.bias_ref, ...), custom_call_target="tpu_custom_call" | custom-call | flops 3221225472 | bytes 3145728 | tf_op jit(solution)/shard_map/attend/pallas_call | solution.py:181
  62.7 5.1 %pair.3 = (bf16[1024,768]{1,0:T(8,128)(2,1)}, bf16[1024,768]{1,0:T(8,128)(2,1)}, bf16[1024,768]{1,0:T(8,128)(2,1)}) custom-call(s32[1]{0:T(128)} %bitcast.me_ref, bf16[512,768]{1,0:T(8,128)(2,1)} %copy-done.2, f32[3,768]{1,0:T(4,128)} %copy-done.41, ...), custom_call_target="tpu_custom_call", output_to_operand_aliasing={{0}: (4, {}), {1}: (5, {}), {2}: (6, {})} | custom-call | flops 1207959552 | bytes 3145728 | tf_op jit(solution)/shard_map/pair/pallas_call | solution.py:129
  67.7 12.0 %attend.3 = (bf16[1024,768]{1,0:T(8,128)(2,1)}, f32[2,6,2,512]{3,2,1,0:T(2,128)}) custom-call(bf16[1024,768]{1,0:T(8,128)(2,1)} %get-tuple-element.280.q_ref, bf16[1024,768]{1,0:T(8,128)(2,1)} %get-tuple-element.385.k_ref, bf16[1024,768]{1,0:T(8,128)(2,1)} %get-tuple-element.386.v_ref, ...), custom_call_target="tpu_custom_call", output_to_operand_aliasing={{0}: (6, {}), {1}: (7, {})} | custom-call | flops 3221225472 | bytes 3145728 | tf_op jit(solution)/shard_map/attend/pallas_call | solution.py:181
  79.7 6.2 %middle.1 = (f32[1024,768]{1,0:T(8,128)}, bf16[1024,768]{1,0:T(8,128)(2,1)}, f32[24,768]{1,0:T(8,128)}) custom-call(bf16[1024,768]{1,0:T(8,128)(2,1)} %bitcast.178, bf16[1024,768]{1,0:T(8,128)(2,1)} %get-tuple-element.306.mixed_ref.o_ref, f32[1024,1]{1,0:T(8,128)} %bitcast.183, bf16[768,768]{1,0:T(8,128)(2,1)} %bitcast.194, f32[1,768]{1,0:T(1,128)} %bo_ref.1, ...), custom_call_target="tpu_custom_call" | custom-call | flops 2415919104 | bytes 7864320 | tf_op jit(solution)/shard_map/middle/pallas_call | solution.py:349
  86.0 14.3 %feed.4 = (f32[1024,768]{1,0:T(8,128)}, f32[1024,768]{1,0:T(8,128)}, f32[24,768]{1,0:T(8,128)}, bf16[2,384,768]{2,1,0:T(8,128)(2,1)}, bf16[2,384,768]{2,1,0:T(8,128)(2,1)}) custom-call(s32[1]{0:T(128)} %bitcast.me_ref, bf16[1024,768]{1,0:T(8,128)(2,1)} %get-tuple-element.348.n2_ref.n2s_ref, bf16[1024,768]{1,0:T(8,128)(2,1)} %bitcast.185, ...), custom_call_target="tpu_custom_call" | custom-call | flops 7247757312 | bytes 15728640 | tf_op jit(solution)/shard_map/feed/pallas_call | solution.py:449
  100.4 16.1 %feed.5 = (f32[1024,768]{1,0:T(8,128)}, f32[1024,768]{1,0:T(8,128)}, f32[24,768]{1,0:T(8,128)}, bf16[2,384,768]{2,1,0:T(8,128)(2,1)}, bf16[2,384,768]{2,1,0:T(8,128)(2,1)}) custom-call(s32[1]{0:T(128)} %bitcast.me_ref, bf16[1024,768]{1,0:T(8,128)(2,1)} %get-tuple-element.348.n2_ref.n2s_ref, ...), custom_call_target="tpu_custom_call", output_to_operand_aliasing={{0}: (9, {}), {1}: (10, {})} | custom-call | flops 7247757312 | bytes 15728640 | tf_op jit(solution)/shard_map/feed/pallas_call | solution.py:449
  118.2 1.5 collective-permute-start.9
  119.7 15.9 %feed.6 = (f32[1024,768]{1,0:T(8,128)}, f32[1024,768]{1,0:T(8,128)}, f32[24,768]{1,0:T(8,128)}, bf16[2,384,768]{2,1,0:T(8,128)(2,1)}, bf16[2,384,768]{2,1,0:T(8,128)(2,1)}) custom-call(s32[1]{0:T(128)} %bitcast.me_ref, bf16[1024,768]{1,0:T(8,128)(2,1)} %get-tuple-element.348.n2_ref.n2s_ref, ...), custom_call_target="tpu_custom_call", output_to_operand_aliasing={{0}: (9, {}), {1}: (10, {})} | custom-call | flops 7247757312 | bytes 15728640 | tf_op jit(solution)/shard_map/feed/pallas_call | solution.py:449
  138.8 16.1 %feed.7 = (f32[1024,768]{1,0:T(8,128)}, f32[1024,768]{1,0:T(8,128)}, f32[24,768]{1,0:T(8,128)}, bf16[2,384,768]{2,1,0:T(8,128)(2,1)}, bf16[2,384,768]{2,1,0:T(8,128)(2,1)}) custom-call(s32[1]{0:T(128)} %bitcast.me_ref, bf16[1024,768]{1,0:T(8,128)(2,1)} %get-tuple-element.348.n2_ref.n2s_ref, ...), custom_call_target="tpu_custom_call", output_to_operand_aliasing={{0}: (9, {}), {1}: (10, {})} | custom-call | flops 7247757312 | bytes 15728640 | tf_op jit(solution)/shard_map/feed/pallas_call | solution.py:449
  154.9 1.9 fusion.6
  159.4 1.6 collective-permute-start.13
  161.6 1.6 collective-permute-start.14
  163.2 12.5 %finish.1 = (bf16[1024,768]{1,0:T(8,128)(2,1)}, f32[1024,768]{1,0:T(8,128)}, bf16[1024,768]{1,0:T(8,128)(2,1)}, f32[24,768]{1,0:T(8,128)}, bf16[2,192,768]{2,1,0:T(8,128)(2,1)}, /*index=5*/bf16[2,192,768]{2,1,0:T(8,128)(2,1)}) custom-call(s32[1]{0:T(128)} %bitcast.me_ref, f32[1024,768]{1,0:T(8,128)} %get-tuple-element.367.feed_ref, ...), custom_call_target="tpu_custom_call" | custom-call | flops 2415919104 | bytes 18874368 | tf_op jit(solution)/shard_map/finish/pallas_call | solution.py:555
  179.0 2.6 collective-permute-start.17
  181.6 16.4 %attend_back.2 = (bf16[1024,384]{1,0:T(8,128)(2,1)}, bf16[1024,384]{1,0:T(8,128)(2,1)}, bf16[1024,384]{1,0:T(8,128)(2,1)}, f32[2,6,64,64]{3,2,1,0:T(8,128)}) custom-call(bf16[1024,768]{1,0:T(8,128)(2,1)} %get-tuple-element.280.q_ref, bf16[1024,768]{1,0:T(8,128)(2,1)} %get-tuple-element.385.k_ref, bf16[1024,768]{1,0:T(8,128)(2,1)} %get-tuple-element.386.v_ref, ...), custom_call_target="tpu_custom_call" | custom-call | flops 8053063680 | bytes 6291456 | tf_op jit(solution)/shard_map/attend_back/pallas_call | solution.py:262
  198.0 1.5 fusion.5
  200.3 1.5 fusion.4
  204.2 1.8 fusion.27
  206.0 1.6 collective-permute-start.19
  208.9 11.2 %weights.2 = (f32[1024,768]{1,0:T(8,128)}, f32[1024,768]{1,0:T(8,128)}, f32[24,768]{1,0:T(8,128)}, bf16[2,576,384]{2,1,0:T(8,128)(2,1)}, bf16[2,576,384]{2,1,0:T(8,128)(2,1)}) custom-call(s32[1]{0:T(128)} %bitcast.me_ref, bf16[1024,768]{1,0:T(8,128)(2,1)} %bitcast.179, bf16[1024,768]{1,0:T(8,128)(2,1)} %copy-done.1, ...), custom_call_target="tpu_custom_call" | custom-call | flops 3623878656 | bytes 18874368 | tf_op jit(solution)/shard_map/weights/pallas_call | solution.py:648
  220.1 1.3 collective-permute-done.19
  221.4 1.4 fusion.20
  224.2 1.6 collective-permute-start.22
  226.2 16.7 %attend_back.3 = (bf16[1024,384]{1,0:T(8,128)(2,1)}, bf16[1024,384]{1,0:T(8,128)(2,1)}, bf16[1024,384]{1,0:T(8,128)(2,1)}, f32[2,6,64,64]{3,2,1,0:T(8,128)}) custom-call(bf16[1024,768]{1,0:T(8,128)(2,1)} %get-tuple-element.280.q_ref, bf16[1024,768]{1,0:T(8,128)(2,1)} %get-tuple-element.385.k_ref, bf16[1024,768]{1,0:T(8,128)(2,1)} %get-tuple-element.386.v_ref, ...), custom_call_target="tpu_custom_call" | custom-call | flops 8053063680 | bytes 6291456 | tf_op jit(solution)/shard_map/attend_back/pallas_call | solution.py:262
  250.6 1.4 collective-permute-start.23
  252.1 1.7 collective-permute-start.24
  253.8 14.0 %weights.3 = (f32[1024,768]{1,0:T(8,128)}, bf16[1024,768]{1,0:T(8,128)(2,1)}, f32[24,768]{1,0:T(8,128)}, bf16[2,576,384]{2,1,0:T(8,128)(2,1)}, bf16[2,576,384]{2,1,0:T(8,128)(2,1)}) custom-call(s32[1]{0:T(128)} %bitcast.me_ref, bf16[1024,768]{1,0:T(8,128)(2,1)} %bitcast.180, bf16[1024,768]{1,0:T(8,128)(2,1)} %copy-done.1, ...), custom_call_target="tpu_custom_call" | custom-call | flops 3623878656 | bytes 18874368 | tf_op jit(solution)/shard_map/weights/pallas_call | solution.py:648
  270.9 1.3 collective-permute-start.27
  273.5 5.2 %collective-permute-done.27 = bf16[2,144,384]{2,1,0:T(8,128)(2,1)S(1)} collective-permute-done((bf16[2,144,384]{2,1,0:T(8,128)(2,1)S(1)}, bf16[2,144,384]{2,1,0:T(8,128)(2,1)S(1)}, u32[]{:S(2)}, u32[]{:S(2)}) %collective-permute-start.27) | collective-permute-done | bytes 221216 | tf_op jit(solution)/shard_map/ppermute | solution.py:693
  279.0 1.6 collective-permute-start.29
  281.1 1.4 collective-permute-start.31
  284.3 8.1 %collective-permute-done.31 = f32[24,768]{1,0:T(8,128)S(1)} collective-permute-done((f32[24,768]{1,0:T(8,128)S(1)}, f32[24,768]{1,0:T(8,128)S(1)}, u32[]{:S(2)}, u32[]{:S(2)}) %collective-permute-start.31) | collective-permute-done | bytes 73760 | tf_op jit(solution)/shard_map/ppermute | solution.py:693
  292.7 1.3 collective-permute-start.32
  295.7 4.8 %collective-permute-done.33 = f32[24,768]{1,0:T(8,128)S(1)} collective-permute-done((f32[24,768]{1,0:T(8,128)S(1)}, f32[24,768]{1,0:T(8,128)S(1)}, u32[]{:S(2)}, u32[]{:S(2)}) %collective-permute-start.33) | collective-permute-done | bytes 73760 | tf_op jit(solution)/shard_map/ppermute | solution.py:693
  300.5 1.3 collective-permute-start.34
  301.9 1.6 collective-permute-start.35
  303.6 14.7 %collective-permute-done.25.gf_ref = bf16[1024,768]{1,0:T(8,128)(2,1)S(1)} collective-permute-done((bf16[1024,768]{1,0:T(8,128)(2,1)S(1)}, bf16[1024,768]{1,0:T(8,128)(2,1)S(1)}, u32[]{:S(2)}, u32[]{:S(2)}) %collective-permute-start.25) | collective-permute-done | bytes 1572896 | tf_op jit(solution)/shard_map/ppermute | solution.py:693
  319.4 6.6 %tokens.1 = f32[1024,768]{1,0:T(8,128)} custom-call(bf16[1024,768]{1,0:T(8,128)(2,1)} %bitcast.181, f32[1,768]{1,0:T(1,128)} %gain_ref.6, f32[1024,768]{1,0:T(8,128)} %get-tuple-element.381.gm_ref, f32[1024,768]{1,0:T(8,128)} %get-tuple-element.452.gq_ref, bf16[1024,768]{1,0:T(8,128)(2,1)} %copy-done.4), custom_call_target="tpu_custom_call" | custom-call | flops 15728640 | bytes 12582912 | tf_op jit(solution)/shard_map/tokens/pallas_call | solution.py:679
  (246 shorter events, 54.2 us)
Async XLA Ops:
  0.7 5.4 %copy-start.44 = (f32[1,768]{1,0:T(1,128)S(1)}, f32[1,768]{1,0:T(1,128)}, u32[]{:S(2)}) copy-start(f32[1,768]{1,0:T(1,128)} %param.37) | copy-start | bytes 9220
  2.8 16.6 %collective-permute-start = (bf16[384,768]{1,0:T(8,128)(2,1)S(1)}, bf16[384,768]{1,0:T(8,128)(2,1)S(1)}, u32[]{:S(2)}, u32[]{:S(2)}) collective-permute-start(bf16[384,768]{1,0:T(8,128)(2,1)S(1)} %select_bitcast_fusion), channel_id=1, source_target_pairs={{0,16},{16,0},{1,17},{17,1},{2,18},{18,2},{3,19},{19,3},{4,20},{20... | collective-permute-start | bytes 1769480 | tf_op jit(solution)/shard_map/ppermute | solution.py:693
  5.8 13.6 %collective-permute-start.1 = (f32[3,768]{1,0:T(4,128)S(1)}, f32[3,768]{1,0:T(4,128)S(1)}, u32[]{:S(2)}, u32[]{:S(2)}) collective-permute-start(f32[3,768]{1,0:T(4,128)S(1)} %pad_maximum_fusion.8), channel_id=1, source_target_pairs={{0,16},{16,0},{1,17},{17,1},{2,18},{18,2},{3,19},{19,3},{4,20},{20... | collective-permute-start | bytes 27656 | tf_op jit(solution)/shard_map/ppermute | solution.py:693
  19.4 24.9 %copy-start.41 = (f32[3,768]{1,0:T(4,128)}, f32[3,768]{1,0:T(4,128)S(1)}, u32[]{:S(2)}) copy-start(f32[3,768]{1,0:T(4,128)S(1)} %collective-permute-done.1.rows_ref) | copy-start | bytes 27652
  20.3 18.7 %collective-permute-start.4 = (bf16[512,768]{1,0:T(8,128)(2,1)S(1)}, bf16[512,768]{1,0:T(8,128)(2,1)S(1)}, u32[]{:S(2)}, u32[]{:S(2)}) collective-permute-start(bf16[512,768]{1,0:T(8,128)(2,1)S(1)} %get-tuple-element.266), channel_id=1, source_target_pairs={{0,16},{16,0},{1,17},{17,1},{2,18},{18,2},{3,19},{19,3},{4,20},{20... | collective-permute-start | bytes 2359304 | tf_op jit(solution)/shard_map/ppermute | solution.py:693
  22.0 14.1 %collective-permute-start.2 = (bf16[384,768]{1,0:T(8,128)(2,1)}, bf16[384,768]{1,0:T(8,128)(2,1)S(1)}, u32[]{:S(2)}, u32[]{:S(2)}) collective-permute-start(bf16[384,768]{1,0:T(8,128)(2,1)} %copy-done.46), channel_id=1, source_target_pairs={{0,2},{1,3},{2,0},{3,1},{4,6},{5,7},{6,4},{7,5},{8,10},{9,11},{10,... | collective-permute-start | bytes 1769480 | tf_op jit(solution)/shard_map/ppermute | solution.py:693
  23.5 12.6 %collective-permute-start.3 = (bf16[384,768]{1,0:T(8,128)(2,1)}, bf16[384,768]{1,0:T(8,128)(2,1)S(1)}, u32[]{:S(2)}, u32[]{:S(2)}) collective-permute-start(bf16[384,768]{1,0:T(8,128)(2,1)} %copy-done.46), channel_id=1, source_target_pairs={{0,1},{1,0},{2,3},{3,2},{4,5},{5,4},{6,7},{7,6},{8,9},{9,8},{10,11... | collective-permute-start | bytes 1769480 | tf_op jit(solution)/shard_map/ppermute | solution.py:693
  36.1 5.7 %copy-start.47 = (bf16[384,768]{1,0:T(8,128)(2,1)}, bf16[384,768]{1,0:T(8,128)(2,1)S(1)}, u32[]{:S(2)}) copy-start(bf16[384,768]{1,0:T(8,128)(2,1)S(1)} %collective-permute-done.2.rest_2_) | copy-start | bytes 1769476
  36.1 5.7 %copy-start.48 = (bf16[384,768]{1,0:T(8,128)(2,1)}, bf16[384,768]{1,0:T(8,128)(2,1)S(1)}, u32[]{:S(2)}) copy-start(bf16[384,768]{1,0:T(8,128)(2,1)S(1)} %collective-permute-done.3.rest_1_) | copy-start | bytes 1769476
  39.0 5.3 %copy-start.22 = (bf16[512,768]{1,0:T(8,128)(2,1)}, bf16[512,768]{1,0:T(8,128)(2,1)S(1)}, u32[]{:S(2)}) copy-start(bf16[512,768]{1,0:T(8,128)(2,1)S(1)} %collective-permute-done.4.x_ref) | copy-start | bytes 2359300
  39.0 2.0 collective-permute-start.5
  41.8 19.9 %collective-permute-start.6 = (bf16[512,768]{1,0:T(8,128)(2,1)S(1)}, bf16[512,768]{1,0:T(8,128)(2,1)S(1)}, u32[]{:S(2)}, u32[]{:S(2)}) collective-permute-start(bf16[512,768]{1,0:T(8,128)(2,1)S(1)} %get-tuple-element.286), channel_id=1, source_target_pairs={{0,16},{16,0},{1,17},{17,1},{2,18},{18,2},{3,19},{19,3},{4,20},{20... | collective-permute-start | bytes 2359304 | tf_op jit(solution)/shard_map/ppermute | solution.py:693
  100.3 17.2 %copy-start.12 = (bf16[2,384,768]{2,1,0:T(8,128)(2,1)S(1)}, bf16[2,384,768]{2,1,0:T(8,128)(2,1)}, u32[]{:S(2)}) copy-start(bf16[2,384,768]{2,1,0:T(8,128)(2,1)} %get-tuple-element.329) | copy-start | bytes 3538948
  100.3 16.2 %collective-permute-start.7 = (bf16[2,384,768]{2,1,0:T(8,128)(2,1)}, bf16[2,384,768]{2,1,0:T(8,128)(2,1)S(1)}, u32[]{:S(2)}, u32[]{:S(2)}) collective-permute-start(bf16[2,384,768]{2,1,0:T(8,128)(2,1)} %get-tuple-element.324), channel_id=1, source_target_pairs={{0,1},{1,0},{2,3},{3,2},{4,5},{5,4},{6,7},{7,6},{8,9},{9,8},{10,11... | collective-permute-start | bytes 3538952 | tf_op jit(solution)/shard_map/ppermute | solution.py:693
  117.7 19.0 %copy-start.10 = (bf16[2,384,768]{2,1,0:T(8,128)(2,1)S(1)}, bf16[2,384,768]{2,1,0:T(8,128)(2,1)}, u32[]{:S(2)}) copy-start(bf16[2,384,768]{2,1,0:T(8,128)(2,1)} %get-tuple-element.346) | copy-start | bytes 3538948
  117.7 18.0 %collective-permute-start.8 = (bf16[2,384,768]{2,1,0:T(8,128)(2,1)}, bf16[2,384,768]{2,1,0:T(8,128)(2,1)S(1)}, u32[]{:S(2)}, u32[]{:S(2)}) collective-permute-start(bf16[2,384,768]{2,1,0:T(8,128)(2,1)} %get-tuple-element.340), channel_id=1, source_target_pairs={{0,1},{1,0},{2,3},{3,2},{4,5},{5,4},{6,7},{7,6},{8,9},{9,8},{10,11... | collective-permute-start | bytes 3538952 | tf_op jit(solution)/shard_map/ppermute | solution.py:693
  118.2 17.4 %collective-permute-start.9 = (bf16[384,768]{1,0:T(8,128)(2,1)S(1)}, bf16[384,768]{1,0:T(8,128)(2,1)S(1)}, u32[]{:S(2)}, u32[]{:S(2)}) collective-permute-start(bf16[384,768]{1,0:T(8,128)(2,1)S(1)} %fusion.11), channel_id=1, source_target_pairs={{0,2},{1,3},{2,0},{3,1},{4,6},{5,7},{6,4},{7,5},{8,10},{9,11},{10,... | collective-permute-start | bytes 1769480 | tf_op jit(solution)/shard_map/ppermute | solution.py:693
  136.8 18.1 %collective-permute-start.10 = (bf16[2,384,768]{2,1,0:T(8,128)(2,1)}, bf16[2,384,768]{2,1,0:T(8,128)(2,1)S(1)}, u32[]{:S(2)}, u32[]{:S(2)}) collective-permute-start(bf16[2,384,768]{2,1,0:T(8,128)(2,1)} %get-tuple-element.357), channel_id=1, source_target_pairs={{0,1},{1,0},{2,3},{3,2},{4,5},{5,4},{6,7},{7,6},{8,9},{9,8},{10,11... | collective-permute-start | bytes 3538952 | tf_op jit(solution)/shard_map/ppermute | solution.py:693
  136.9 18.0 %collective-permute-start.11 = (bf16[384,768]{1,0:T(8,128)(2,1)S(1)}, bf16[384,768]{1,0:T(8,128)(2,1)}, u32[]{:S(2)}, u32[]{:S(2)}) collective-permute-start(bf16[384,768]{1,0:T(8,128)(2,1)S(1)} %fusion.12), channel_id=1, source_target_pairs={{0,2},{1,3},{2,0},{3,1},{4,6},{5,7},{6,4},{7,5},{8,10},{9,11},{10,... | collective-permute-start | bytes 1769480 | tf_op jit(solution)/shard_map/ppermute | solution.py:693
  159.2 16.5 %collective-permute-start.12 = (bf16[2,384,768]{2,1,0:T(8,128)(2,1)}, bf16[2,384,768]{2,1,0:T(8,128)(2,1)}, u32[]{:S(2)}, u32[]{:S(2)}) collective-permute-start(bf16[2,384,768]{2,1,0:T(8,128)(2,1)} %get-tuple-element.377), channel_id=1, source_target_pairs={{0,1},{1,0},{2,3},{3,2},{4,5},{5,4},{6,7},{7,6},{8,9},{9,8},{10,11... | collective-permute-start | bytes 3538952 | tf_op jit(solution)/shard_map/ppermute | solution.py:693
  159.4 16.3 %collective-permute-start.13 = (bf16[384,768]{1,0:T(8,128)(2,1)}, bf16[384,768]{1,0:T(8,128)(2,1)}, u32[]{:S(2)}, u32[]{:S(2)}) collective-permute-start(bf16[384,768]{1,0:T(8,128)(2,1)} %fusion.13), channel_id=1, source_target_pairs={{0,2},{1,3},{2,0},{3,1},{4,6},{5,7},{6,4},{7,5},{8,10},{9,11},{10,... | collective-permute-start | bytes 1769480 | tf_op jit(solution)/shard_map/ppermute | solution.py:693
  161.6 14.1 %collective-permute-start.14 = (bf16[2,96,768]{2,1,0:T(8,128)(2,1)}, bf16[2,96,768]{2,1,0:T(8,128)(2,1)S(1)}, u32[]{:S(2)}, u32[]{:S(2)}) collective-permute-start(bf16[2,96,768]{2,1,0:T(8,128)(2,1)} %slice.333), channel_id=1, source_target_pairs={{0,4},{1,5},{2,6},{3,7},{4,0},{5,1},{6,2},{7,3},{8,12},{9,13},{10,... | collective-permute-start | bytes 884744 | tf_op jit(solution)/shard_map/ppermute | solution.py:693
  178.3 22.0 %collective-permute-start.15 = (bf16[2,192,768]{2,1,0:T(8,128)(2,1)}, bf16[2,192,768]{2,1,0:T(8,128)(2,1)}, u32[]{:S(2)}, u32[]{:S(2)}) collective-permute-start(bf16[2,192,768]{2,1,0:T(8,128)(2,1)} %get-tuple-element.398), channel_id=1, source_target_pairs={{0,1},{1,0},{2,3},{3,2},{4,5},{5,4},{6,7},{7,6},{8,9},{9,8},{10,11... | collective-permute-start | bytes 1769480 | tf_op jit(solution)/shard_map/ppermute | solution.py:693
  178.3 21.9 %collective-permute-start.16 = (bf16[384,768]{1,0:T(8,128)(2,1)S(1)}, bf16[384,768]{1,0:T(8,128)(2,1)}, u32[]{:S(2)}, u32[]{:S(2)}) collective-permute-start(bf16[384,768]{1,0:T(8,128)(2,1)S(1)} %fusion.16), channel_id=1, source_target_pairs={{0,2},{1,3},{2,0},{3,1},{4,6},{5,7},{6,4},{7,5},{8,10},{9,11},{10,... | collective-permute-start | bytes 1769480 | tf_op jit(solution)/shard_map/ppermute | solution.py:693
  179.0 21.2 %collective-permute-start.17 = (bf16[96,768]{1,0:T(8,128)(2,1)S(1)}, bf16[96,768]{1,0:T(8,128)(2,1)S(1)}, u32[]{:S(2)}, u32[]{:S(2)}) collective-permute-start(bf16[96,768]{1,0:T(8,128)(2,1)S(1)} %slice_bitcast_fusion.12), channel_id=1, source_target_pairs={{0,8},{1,9},{2,10},{3,11},{4,12},{5,13},{6,14},{7,15},{8,0},{9,1},... | collective-permute-start | bytes 442376 | tf_op jit(solution)/shard_map/ppermute | solution.py:693
  206.0 15.3 %collective-permute-start.19 = (bf16[2,192,768]{2,1,0:T(8,128)(2,1)}, bf16[2,192,768]{2,1,0:T(8,128)(2,1)S(1)}, u32[]{:S(2)}, u32[]{:S(2)}) collective-permute-start(bf16[2,192,768]{2,1,0:T(8,128)(2,1)} %slice.348), channel_id=1, source_target_pairs={{0,4},{1,5},{2,6},{3,7},{4,0},{5,1},{6,2},{7,3},{8,12},{9,13},{10,... | collective-permute-start | bytes 1769480 | tf_op jit(solution)/shard_map/ppermute | solution.py:693
  207.7 12.3 %collective-permute-start.18 = (bf16[192,768]{1,0:T(8,128)(2,1)}, bf16[192,768]{1,0:T(8,128)(2,1)S(1)}, u32[]{:S(2)}, u32[]{:S(2)}) collective-permute-start(bf16[192,768]{1,0:T(8,128)(2,1)} %fusion.27), channel_id=1, source_target_pairs={{0,2},{1,3},{2,0},{3,1},{4,6},{5,7},{6,4},{7,5},{8,10},{9,11},{10,... | collective-permute-start | bytes 884744 | tf_op jit(solution)/shard_map/ppermute | solution.py:693
  224.1 19.0 %collective-permute-start.20 = (bf16[2,576,384]{2,1,0:T(8,128)(2,1)}, bf16[2,576,384]{2,1,0:T(8,128)(2,1)S(1)}, u32[]{:S(2)}, u32[]{:S(2)}) collective-permute-start(bf16[2,576,384]{2,1,0:T(8,128)(2,1)} %get-tuple-element.428), channel_id=1, source_target_pairs={{0,1},{1,0},{2,3},{3,2},{4,5},{5,4},{6,7},{7,6},{8,9},{9,8},{10,11... | collective-permute-start | bytes 2654216 | tf_op jit(solution)/shard_map/ppermute | solution.py:693
  224.2 18.9 %collective-permute-start.22 = (bf16[2,144,768]{2,1,0:T(8,128)(2,1)S(1)}, bf16[2,144,768]{2,1,0:T(8,128)(2,1)S(1)}, u32[]{:S(2)}, u32[]{:S(2)}) collective-permute-start(bf16[2,144,768]{2,1,0:T(8,128)(2,1)S(1)} %slice.355), channel_id=1, source_target_pairs={{0,4},{1,5},{2,6},{3,7},{4,0},{5,1},{6,2},{7,3},{8,12},{9,13},{10,... | collective-permute-start | bytes 1327112 | tf_op jit(solution)/shard_map/ppermute | solution.py:693
  225.8 17.0 %collective-permute-start.21 = (bf16[192,768]{1,0:T(8,128)(2,1)S(1)}, bf16[192,768]{1,0:T(8,128)(2,1)S(1)}, u32[]{:S(2)}, u32[]{:S(2)}) collective-permute-start(bf16[192,768]{1,0:T(8,128)(2,1)S(1)} %slice_bitcast_fusion.3), channel_id=1, source_target_pairs={{0,8},{1,9},{2,10},{3,11},{4,12},{5,13},{6,14},{7,15},{8,0},{9,1},... | collective-permute-start | bytes 884744 | tf_op jit(solution)/shard_map/ppermute | solution.py:693
  250.6 17.2 %collective-permute-start.23 = (bf16[576,384]{1,0:T(8,128)(2,1)}, bf16[576,384]{1,0:T(8,128)(2,1)S(1)}, u32[]{:S(2)}, u32[]{:S(2)}) collective-permute-start(bf16[576,384]{1,0:T(8,128)(2,1)} %fusion.22), channel_id=1, source_target_pairs={{0,2},{1,3},{2,0},{3,1},{4,6},{5,7},{6,4},{7,5},{8,10},{9,11},{10,... | collective-permute-start | bytes 1327112 | tf_op jit(solution)/shard_map/ppermute | solution.py:693
  252.1 16.5 %copy-start.21 = (bf16[2,576,384]{2,1,0:T(8,128)(2,1)S(1)}, bf16[2,576,384]{2,1,0:T(8,128)(2,1)}, u32[]{:S(2)}) copy-start(bf16[2,576,384]{2,1,0:T(8,128)(2,1)} %copy-done.19) | copy-start | bytes 2654212
  252.1 15.6 %collective-permute-start.24 = (bf16[144,768]{1,0:T(8,128)(2,1)}, bf16[144,768]{1,0:T(8,128)(2,1)S(1)}, u32[]{:S(2)}, u32[]{:S(2)}) collective-permute-start(bf16[144,768]{1,0:T(8,128)(2,1)} %slice_bitcast_fusion.9), channel_id=1, source_target_pairs={{0,8},{1,9},{2,10},{3,11},{4,12},{5,13},{6,14},{7,15},{8,0},{9,1},... | collective-permute-start | bytes 663560 | tf_op jit(solution)/shard_map/ppermute | solution.py:693
  270.7 8.1 %collective-permute-start.26 = (bf16[2,576,384]{2,1,0:T(8,128)(2,1)}, bf16[2,576,384]{2,1,0:T(8,128)(2,1)S(1)}, u32[]{:S(2)}, u32[]{:S(2)}) collective-permute-start(bf16[2,576,384]{2,1,0:T(8,128)(2,1)} %get-tuple-element.459), channel_id=1, source_target_pairs={{0,1},{1,0},{2,3},{3,2},{4,5},{5,4},{6,7},{7,6},{8,9},{9,8},{10,11... | collective-permute-start | bytes 2654216 | tf_op jit(solution)/shard_map/ppermute | solution.py:693
  270.9 8.0 %copy-start.17 = (bf16[2,576,384]{2,1,0:T(8,128)(2,1)S(1)}, bf16[2,576,384]{2,1,0:T(8,128)(2,1)}, u32[]{:S(2)}) copy-start(bf16[2,576,384]{2,1,0:T(8,128)(2,1)} %get-tuple-element.463) | copy-start | bytes 2654212
  270.9 7.8 %collective-permute-start.27 = (bf16[2,144,384]{2,1,0:T(8,128)(2,1)S(1)}, bf16[2,144,384]{2,1,0:T(8,128)(2,1)S(1)}, u32[]{:S(2)}, u32[]{:S(2)}) collective-permute-start(bf16[2,144,384]{2,1,0:T(8,128)(2,1)S(1)} %slice.365), channel_id=1, source_target_pairs={{0,4},{1,5},{2,6},{3,7},{4,0},{5,1},{6,2},{7,3},{8,12},{9,13},{10,... | collective-permute-start | bytes 663560 | tf_op jit(solution)/shard_map/ppermute | solution.py:693
  272.3 1.3 collective-permute-start.28
  273.3 7.3 %copy-start.37 = (bf16[144,768]{1,0:T(8,128)(2,1)S(1)}, bf16[144,768]{1,0:T(8,128)(2,1)}, u32[]{:S(2)}) copy-start(bf16[144,768]{1,0:T(8,128)(2,1)} %copy-done.36) | copy-start | bytes 663556
  279.0 13.4 %collective-permute-start.29 = (bf16[576,384]{1,0:T(8,128)(2,1)S(1)}, bf16[576,384]{1,0:T(8,128)(2,1)S(1)}, u32[]{:S(2)}, u32[]{:S(2)}) collective-permute-start(bf16[576,384]{1,0:T(8,128)(2,1)S(1)} %fusion.24), channel_id=1, source_target_pairs={{0,2},{1,3},{2,0},{3,1},{4,6},{5,7},{6,4},{7,5},{8,10},{9,11},{10,... | collective-permute-start | bytes 1327112 | tf_op jit(solution)/shard_map/ppermute | solution.py:693
  280.6 11.7 %collective-permute-start.30 = (bf16[144,384]{1,0:T(8,128)(2,1)S(1)}, bf16[144,384]{1,0:T(8,128)(2,1)S(1)}, u32[]{:S(2)}, u32[]{:S(2)}) collective-permute-start(bf16[144,384]{1,0:T(8,128)(2,1)S(1)} %slice_bitcast_fusion.16), channel_id=1, source_target_pairs={{0,8},{1,9},{2,10},{3,11},{4,12},{5,13},{6,14},{7,15},{8,0},{9,1},... | collective-permute-start | bytes 331784 | tf_op jit(solution)/shard_map/ppermute | solution.py:693
  281.1 11.3 %collective-permute-start.31 = (f32[24,768]{1,0:T(8,128)S(1)}, f32[24,768]{1,0:T(8,128)S(1)}, u32[]{:S(2)}, u32[]{:S(2)}) collective-permute-start(f32[24,768]{1,0:T(8,128)S(1)} %fusion.48), channel_id=1, source_target_pairs={{0,2},{1,3},{2,0},{3,1},{4,6},{5,7},{6,4},{7,5},{8,10},{9,11},{10,... | collective-permute-start | bytes 221192 | tf_op jit(solution)/shard_map/ppermute | solution.py:693
  283.2 35.1 %collective-permute-start.25 = (bf16[1024,768]{1,0:T(8,128)(2,1)S(1)}, bf16[1024,768]{1,0:T(8,128)(2,1)S(1)}, u32[]{:S(2)}, u32[]{:S(2)}) collective-permute-start(bf16[1024,768]{1,0:T(8,128)(2,1)S(1)} %copy-done.45), channel_id=1, source_target_pairs={{0,16},{16,0},{1,17},{17,1},{2,18},{18,2},{3,19},{19,3},{4,20},{20... | collective-permute-start | bytes 4718600 | tf_op jit(solution)/shard_map/ppermute | solution.py:693
  292.7 7.7 %collective-permute-start.32 = (bf16[2,144,384]{2,1,0:T(8,128)(2,1)S(1)}, bf16[2,144,384]{2,1,0:T(8,128)(2,1)S(1)}, u32[]{:S(2)}, u32[]{:S(2)}) collective-permute-start(bf16[2,144,384]{2,1,0:T(8,128)(2,1)S(1)} %slice.375), channel_id=1, source_target_pairs={{0,4},{1,5},{2,6},{3,7},{4,0},{5,1},{6,2},{7,3},{8,12},{9,13},{10,... | collective-permute-start | bytes 663560 | tf_op jit(solution)/shard_map/ppermute | solution.py:693
  294.1 6.4 %collective-permute-start.33 = (f32[24,768]{1,0:T(8,128)S(1)}, f32[24,768]{1,0:T(8,128)S(1)}, u32[]{:S(2)}, u32[]{:S(2)}) collective-permute-start(f32[24,768]{1,0:T(8,128)S(1)} %add.257), channel_id=1, source_target_pairs={{0,4},{1,5},{2,6},{3,7},{4,0},{5,1},{6,2},{7,3},{8,12},{9,13},{10,... | collective-permute-start | bytes 221192 | tf_op jit(solution)/shard_map/ppermute | solution.py:693
  300.5 25.6 %collective-permute-start.34 = (bf16[144,384]{1,0:T(8,128)(2,1)S(1)}, bf16[144,384]{1,0:T(8,128)(2,1)S(1)}, u32[]{:S(2)}, u32[]{:S(2)}) collective-permute-start(bf16[144,384]{1,0:T(8,128)(2,1)S(1)} %slice_bitcast_fusion.15), channel_id=1, source_target_pairs={{0,8},{1,9},{2,10},{3,11},{4,12},{5,13},{6,14},{7,15},{8,0},{9,1},... | collective-permute-start | bytes 331784 | tf_op jit(solution)/shard_map/ppermute | solution.py:693
  301.9 24.2 %collective-permute-start.35 = (f32[24,768]{1,0:T(8,128)S(1)}, f32[24,768]{1,0:T(8,128)S(1)}, u32[]{:S(2)}, u32[]{:S(2)}) collective-permute-start(f32[24,768]{1,0:T(8,128)S(1)} %add.260), channel_id=1, source_target_pairs={{0,8},{1,9},{2,10},{3,11},{4,12},{5,13},{6,14},{7,15},{8,0},{9,1},... | collective-permute-start | bytes 221192 | tf_op jit(solution)/shard_map/ppermute | solution.py:693
  327.5 5.8 %collective-permute-start.37 = (bf16[96,768]{1,0:T(8,128)(2,1)S(1)}, bf16[96,768]{1,0:T(8,128)(2,1)S(1)}, u32[]{:S(2)}, u32[]{:S(2)}) collective-permute-start(bf16[96,768]{1,0:T(8,128)(2,1)S(1)} %fusion.29), channel_id=1, source_target_pairs={{0,16},{16,0},{1,17},{17,1},{2,18},{18,2},{3,19},{19,3},{4,20},{20... | collective-permute-start | bytes 442376 | tf_op jit(solution)/shard_map/ppermute | solution.py:693
  328.7 4.0 %collective-permute-start.36 = (f32[3,48]{1,0:T(4,128)S(1)}, f32[3,48]{1,0:T(4,128)S(1)}, u32[]{:S(2)}, u32[]{:S(2)}) collective-permute-start(f32[3,48]{1,0:T(4,128)S(1)} %dynamic-slice.3), channel_id=1, source_target_pairs={{0,16},{16,0},{1,17},{17,1},{2,18},{18,2},{3,19},{19,3},{4,20},{20... | collective-permute-start | bytes 1736 | tf_op jit(solution)/shard_map/ppermute | solution.py:693
  (40 other events, 69.9 us)
